TPU v7x, 32 devices: a whole 2x2x4 slice. The times are simulated.
32 devices in a mesh: seq: 4 (over y, core), head: 8 (over z, x).
Axes of the slice: x: 2, y: 2, z: 4, core: 2. Of those that a mesh axis runs over, the one named last changes fastest.
Arguments:
- query_rows: float32 [2, 8192, 1024], P(None, 'seq', 'head'), may hold values from -0.5 to 0.5
- key_rows: float32 [2, 8192, 1024], P(None, 'seq', 'head'), may hold values from -6 to 6
- value_rows: float32 [2, 8192, 1024], P(None, 'seq', 'head'), may hold values from -6 to 6
- cotangent: float32 [2, 8192, 1024], P(None, 'seq', 'head'), may hold values from -6 to 6
- selector: int32 [2, 8, 8192], P(None, 'head', 'seq'), may hold values from 0 to 15
- level_table: float32 [16, 3], replicated, may hold values from 0.05 to 1
- span_length: int32 [2, 4], P(None, 'seq'), may hold values from 1024 to 2048
- norm_gain: float32 [1024], P('head'), may hold values from 0.1 to 1.9
Outputs:
- attended: float32 [2, 8192, 1024], P(None, 'seq', 'head')
- state_gradient: float32 [2, 4, 128, 1024], P(None, 'seq', None, 'head')
Inputs may be any that keep to these rules, and one draw needn't show every extreme that they name: Keys at positions span_length and later of a block are padding.
All inputs are finite; a program needn't handle non-finite values.
Results may differ from a plain program's by a relative error of at most 0.0001.
Values sent between devices are 32-bit elements; how exact they have to be, the bound alone decides.
No kernel may reach another device: no remote copies, remote signals or barrier semaphores. Data moves between devices by JAX's collectives and lax.ppermute only.
A program may use at most 128 MiB of HBM per device.

v0:
```python
import functools

import jax
import jax.numpy as jnp
from jax import lax
from jax.experimental import pallas as pl
from jax.experimental.pallas import tpu as pltpu
from jax.sharding import PartitionSpec as P

DH = 128
LANES = 128
CHUNK = 256
LOAD = 512
EPSILON = 1e-06
GRANT = 8 << 20
F32, BF16 = jnp.float32, jnp.bfloat16
NN = (((1,), (0,)), ((), ()))
NT = (((1,), (1,)), ((), ()))
VMEM = pl.BlockSpec(memory_space=pltpu.VMEM)
SMEM = pl.BlockSpec(memory_space=pltpu.SMEM)
HBM = pl.BlockSpec(memory_space=pl.ANY)


def dot(left, right, dims=NN):
    return lax.dot_general(left, right, dims, preferred_element_type=F32)


def halves(array):
    high = array.astype(BF16)
    return high, (array - high.astype(F32)).astype(BF16)


def chunk_states(groups, tokens, spans, key_at, value_at, outs, ready=None):
    key_out, value_out, prefix_out, state_out = outs
    spots = [(group, chunk) for group in range(groups) for chunk in range(tokens // CHUNK)]

    def prepare(group, chunk):
        if ready is not None:
            ready(group, chunk)
        rows = pl.ds(chunk * CHUNK, CHUNK)
        position = chunk * CHUNK + lax.broadcasted_iota(jnp.int32, (CHUNK, DH), 0)
        live = jnp.where(position < spans[group], key_at(group, rows), 0.0)
        key_out[group, rows, :] = jnp.concatenate(halves(live), axis=1)
        value_out[group, :, rows] = jnp.concatenate(halves(value_at(group, rows).T), axis=0)

    prepare(*spots[0])
    total = None
    for index, (group, chunk) in enumerate(spots):
        if index + 1 < len(spots):
            prepare(*spots[index + 1])
        rows = pl.ds(chunk * CHUNK, CHUNK)
        total = jnp.zeros((DH, DH), F32) if chunk == 0 else total
        prefix_out[group, chunk] = jnp.concatenate(halves(total), axis=1)
        square = dot(value_out[group, :, rows], key_out[group, rows, :])
        square = square[:DH] + square[DH:]
        total = total + (square[:, :DH] + square[:, DH:])
        if chunk == tokens // CHUNK - 1:
            state_out[group] = total


def state_kernel(heads, span_hbm, key_hbm, value_hbm, *refs):
    *outs, span_ref, key_ref, value_ref, span_sem, sems = refs
    groups, tokens, _ = key_ref.shape
    span_copy = pltpu.make_async_copy(span_hbm, span_ref, span_sem)
    span_copy.start()
    loads = {}
    for group in range(groups):
        for load in range(tokens // LOAD):
            rows = pl.ds(load * LOAD, LOAD)
            loads[group, load] = [
                pltpu.make_async_copy(
                    source.at[group, rows], target.at[group, rows], sems.at[kind, group, load]
                )
                for kind, (source, target) in enumerate(
                    ((key_hbm, key_ref), (value_hbm, value_ref))
                )
            ]
            for copy in loads[group, load]:
                copy.start()
    span_copy.wait()

    def ready(group, chunk):
        if chunk * CHUNK % LOAD == 0:
            for copy in loads[group, chunk * CHUNK // LOAD]:
                copy.wait()

    chunk_states(
        groups,
        tokens,
        [span_ref[group // heads] for group in range(groups)],
        lambda group, rows: key_ref[group, rows, :],
        lambda group, rows: value_ref[group, rows, :],
        outs,
        ready,
    )


def token_kernel(heads, table_ref, selector_ref, cotangent_ref, gain_ref, weight_out, scaled_out):
    groups, tokens, _ = cotangent_ref.shape
    levels, choices = table_ref.shape
    for group in range(groups):
        gain = gain_ref[pl.ds(group % heads, 1), :]
        for chunk in range(tokens // CHUNK):
            rows = pl.ds(chunk * CHUNK, CHUNK)
            scaled_out[group, :, rows] = (cotangent_ref[group, rows, :] * gain).T
    for group in range(groups):
        selector = selector_ref[group]
        for level in range(levels):
            weight = jnp.zeros(selector.shape, F32)
            for choice in range(choices):
                weight = jnp.where(selector == choice, table_ref[level, choice], weight)
            weight_out[level, group] = weight


def causal_halves(scores, ahead):
    strips = []
    for row in range(0, CHUNK, LANES):
        blocks = []
        for column in range(0, CHUNK, LANES):
            block = scores[row : row + LANES, column : column + LANES]
            if row == column:
                block = jnp.where(ahead, block, 0.0)
            zero = jnp.zeros(block.shape, BF16)
            blocks.append((zero, zero) if row > column else halves(block))
        strips.append([jnp.concatenate(parts, axis=1) for parts in zip(*blocks)])
    return [jnp.concatenate(parts, axis=0) for parts in zip(*strips)]


def local_kernel(weight_ref, query_ref, key_ref, value_ref, prefix_ref, *refs):
    high_out, low_out, local_out, high_own, low_own = refs
    groups, tokens, _ = query_ref.shape
    levels = weight_ref.shape[0]
    ahead = lax.broadcasted_iota(jnp.int32, (LANES, LANES), 0) <= lax.broadcasted_iota(
        jnp.int32, (LANES, LANES), 1
    )
    spots = [(group, chunk) for group in range(groups) for chunk in range(tokens // CHUNK)]

    def prepare(index):
        group, chunk = spots[index]
        rows = pl.ds(chunk * CHUNK, CHUNK)
        query = query_ref[group, rows, :].T
        high_own[index % 2], low_own[index % 2] = halves(
            query * token_row(weight_ref.at[0, group], chunk)
        )
        for level in range(1, levels):
            high, low = halves(query * token_row(weight_ref.at[level, group], chunk))
            high_out[group, pl.ds((level - 1) * DH, DH), rows] = high
            low_out[group, pl.ds((level - 1) * DH, DH), rows] = low

    prepare(0)
    for index, (group, chunk) in enumerate(spots):
        if index + 1 < len(spots):
            prepare(index + 1)
        rows = pl.ds(chunk * CHUNK, CHUNK)
        high, low = high_own[index % 2], low_own[index % 2]
        left = jnp.concatenate([key_ref[group, rows, :], prefix_ref[group, chunk]], axis=0)
        mixed = dot(left, jnp.concatenate([high, high], axis=0)) + dot(left[:, :DH], low)
        scores_high, scores_low = causal_halves(mixed[:CHUNK], ahead)
        values = value_ref[group, :, rows]
        near = dot(values, scores_high)
        near = near[:DH] + near[DH:] + dot(values[:DH], scores_low)
        local_out[group, :, rows] = near + mixed[CHUNK:]


def combine_kernel(
    heads, local_ref, high_ref, low_ref, scaled_ref, *refs
):
    *bucket_refs, combined_out, sums_out = refs
    groups, _, tokens = local_ref.shape
    seq_index = lax.axis_index("seq")
    per = CHUNK // LANES
    for group in range(groups):
        buckets = []
        for level, bucket_ref in enumerate(bucket_refs):
            reads = seq_index >> level & 1
            buckets.append(jnp.where(reads == 1, bucket_ref[group], 0.0))
        bucket_high, bucket_low = halves(jnp.concatenate(buckets, axis=1))
        both = jnp.concatenate([bucket_high, bucket_low], axis=0)
        for chunk in range(tokens // CHUNK):
            rows = pl.ds(chunk * CHUNK, CHUNK)
            square = dot(both, high_ref[group, :, rows])
            square = square[:DH] + square[DH:] + dot(bucket_high, low_ref[group, :, rows])
            combined = square + local_ref[group, :, rows]
            combined_out[group, :, rows] = combined
            sums = (
                jnp.sum(combined * combined, axis=0, keepdims=True),
                jnp.sum(combined * scaled_ref[group, :, rows], axis=0, keepdims=True),
            )
            for kind in range(2):
                for part in range(per):
                    spot = (kind, group // heads, pl.ds(chunk * per + part, 1))
                    row = sums[kind][:, part * LANES : (part + 1) * LANES]
                    sums_out[spot] = row if group % heads == 0 else sums_out[spot] + row


def factors(sums_ref, batch, full_width):
    inverse = lax.rsqrt(sums_ref[0, batch] / full_width + EPSILON)
    return inverse, inverse * inverse * inverse * sums_ref[1, batch] / full_width


def token_row(array, chunk):
    per = CHUNK // LANES
    spots = range(chunk * per, (chunk + 1) * per)
    return jnp.concatenate([array[spot : spot + 1, :] for spot in spots], axis=1)


def fold(total):
    total = total[:DH] + total[DH:]
    return (total[:, :DH] + total[:, DH:]).T


def top_gradient_kernel(
    heads, full_width, sums_ref, combined_ref, scaled_ref, high_ref, low_ref, *outs
):
    grad_out, parts_out = outs
    groups, _, tokens = combined_ref.shape
    level = high_ref.shape[1] // DH - 1
    top = pl.ds(level * DH, DH)
    reads = lax.axis_index("seq") >> level & 1
    for group in range(groups):
        inverse, pull = factors(sums_ref, group // heads, full_width)
        total = jnp.zeros((2 * DH, 2 * DH), F32)
        for chunk in range(tokens // CHUNK):
            rows = pl.ds(chunk * CHUNK, CHUNK)
            grad = scaled_ref[group, :, rows] * token_row(inverse, chunk) - combined_ref[
                group, :, rows
            ] * token_row(pull, chunk)
            both = jnp.concatenate(halves(grad), axis=0)
            parts_out[group, :, rows] = both
            weighted = jnp.concatenate([high_ref[group, top, rows], low_ref[group, top, rows]], 0)
            total = total + dot(both, weighted, NT)
        grad_out[group] = jnp.where(reads == 1, fold(total), 0.0)


def rest_gradient_kernel(parts_ref, high_ref, low_ref, *grad_outs):
    groups, _, tokens = parts_ref.shape
    for level, grad_out in enumerate(grad_outs):
        spot = pl.ds(level * DH, DH)
        reads = lax.axis_index("seq") >> level & 1
        for group in range(groups):
            total = jnp.zeros((2 * DH, 2 * DH), F32)
            for chunk in range(tokens // CHUNK):
                rows = pl.ds(chunk * CHUNK, CHUNK)
                weighted = jnp.concatenate(
                    [high_ref[group, spot, rows], low_ref[group, spot, rows]], 0
                )
                total = total + dot(parts_ref[group, :, rows], weighted, NT)
            grad_out[group] = jnp.where(reads == 1, fold(total), 0.0)


def finish_kernel(*refs):
    *part_refs, out_ref = refs
    total = part_refs[0][...]
    for part_ref in part_refs[1:]:
        total = total + part_ref[...]
    out_ref[...] = total


def attended_kernel(
    heads, full_width, sums_ref, combined_ref, gain_ref, attended_hbm, attended_ref, sems
):
    groups, _, tokens = combined_ref.shape
    copies = []
    for group in range(groups):
        gain = gain_ref[pl.ds(group % heads, 1), :]
        inverse, _ = factors(sums_ref, group // heads, full_width)
        for chunk in range(tokens // CHUNK):
            rows = pl.ds(chunk * CHUNK, CHUNK)
            scaled = combined_ref[group, :, rows] * token_row(inverse, chunk)
            attended_ref[group, rows, :] = scaled.T * gain
            if (chunk + 1) * CHUNK % LOAD == 0:
                load = (chunk + 1) * CHUNK // LOAD - 1
                rows = pl.ds(load * LOAD, LOAD)
                copies.append(
                    pltpu.make_async_copy(
                        attended_ref.at[group, rows],
                        attended_hbm.at[group, rows],
                        sems.at[group, load],
                    )
                )
                copies[-1].start()
    for copy in copies:
        copy.wait()


def resident(shape, dtype=F32):
    return pltpu.VMEM(shape, dtype)


def keep(array):
    return pltpu.with_memory_space_constraint(array, pltpu.VMEM)


def leave(array):
    return pltpu.with_memory_space_constraint(array, pltpu.HBM)


def partner(shard, axis, stride):
    return lax.ppermute(shard, axis, [(i, i ^ 1 << stride) for i in range(lax.axis_size(axis))])


def exchange(shard, axis, masks):
    size = lax.axis_size(axis)
    others = [lax.ppermute(shard, axis, [(i, i ^ mask) for i in range(size)]) for mask in masks]
    return sum(others, shard)


def body(
    query_rows, key_rows, value_rows, cotangent, selector, level_table, span_length, norm_gain
):
    batch_count, tokens, local_width = query_rows.shape
    heads = local_width // DH
    groups = batch_count * heads
    full_width = local_width * lax.axis_size("head")
    level_count = lax.axis_size("seq").bit_length() - 1

    def split(rows):
        rows = rows.reshape(batch_count, tokens, heads, DH)
        return rows.transpose(0, 2, 1, 3).reshape(groups, tokens, DH)

    queries, keys, values, cotangents = map(split, (query_rows, key_rows, value_rows, cotangent))
    selectors = selector.reshape(groups, tokens // LANES, LANES)
    gains = norm_gain.reshape(heads, DH)
    chunks = tokens // CHUNK
    stacked = level_count * DH
    call = functools.partial(
        pl.pallas_call, compiler_params=pltpu.CompilerParams(vmem_limit_bytes=GRANT)
    )

    key_parts, value_parts, prefixes, state = call(
        functools.partial(state_kernel, heads),
        out_shape=(
            resident((groups, tokens, 2 * DH), BF16),
            resident((groups, 2 * DH, tokens), BF16),
            resident((groups, chunks, DH, 2 * DH), BF16),
            resident((groups, DH, DH)),
        ),
        in_specs=[HBM] * 3,
        out_specs=(VMEM,) * 4,
        scratch_shapes=[
            pltpu.SMEM((batch_count,), jnp.int32),
            pltpu.VMEM((groups, tokens, DH), F32),
            pltpu.VMEM((groups, tokens, DH), F32),
            pltpu.SemaphoreType.DMA(()),
            pltpu.SemaphoreType.DMA((2, groups, tokens // LOAD)),
        ],
        name="state",
    )(*map(leave, (span_length.reshape(batch_count), keys, values)))
    state, queries, cotangents, gains, selectors, level_table = lax.optimization_barrier(
        (state, queries, cotangents, gains, selectors, level_table)
    )

    weights, scaled = call(
        functools.partial(token_kernel, heads),
        out_shape=(
            resident((level_count + 1, groups, tokens // LANES, LANES)),
            resident((groups, DH, tokens)),
        ),
        in_specs=[SMEM] + [VMEM] * 3,
        out_specs=(VMEM,) * 2,
        name="token",
    )(level_table.T, selectors, cotangents, gains)

    buckets = []
    pending = state
    for level in range(level_count):
        buckets.append(partner(pending, "seq", level))
        pending = pending + buckets[-1]

    weighted_high, weighted_low, local_sum = call(
        local_kernel,
        out_shape=(
            resident((groups, stacked, tokens), BF16),
            resident((groups, stacked, tokens), BF16),
            resident((groups, DH, tokens)),
        ),
        in_specs=[VMEM] * 5,
        out_specs=(VMEM,) * 3,
        scratch_shapes=[pltpu.VMEM((2, DH, CHUNK), BF16)] * 2,
        name="local",
    )(*map(keep, (weights, queries, key_parts, value_parts, prefixes)))

    combined, sums = call(
        functools.partial(combine_kernel, heads),
        out_shape=(
            resident((groups, DH, tokens)),
            resident((2, batch_count, tokens // LANES, LANES)),
        ),
        in_specs=[VMEM] * (4 + level_count),
        out_specs=(VMEM,) * 2,
        name="combine",
    )(*map(keep, (local_sum, weighted_high, weighted_low, scaled, *buckets)))

    head_bits = lax.axis_size("head").bit_length() - 1
    sums = exchange(sums, "head", range(1, 1 << min(2, head_bits)))
    for level in range(2, head_bits):
        sums = exchange(sums, "head", (1 << level,))

    top_grad, grad_parts = call(
        functools.partial(top_gradient_kernel, heads, full_width),
        out_shape=(resident((groups, DH, DH)), resident((groups, 2 * DH, tokens), BF16)),
        in_specs=[VMEM] * 5,
        out_specs=(VMEM,) * 2,
        name="top_gradient",
    )(*map(keep, (sums, combined, scaled, weighted_high, weighted_low)))
    grads = call(
        rest_gradient_kernel,
        out_shape=(resident((groups, DH, DH)),) * (level_count - 1),
        in_specs=[VMEM] * 3,
        out_specs=(VMEM,) * (level_count - 1),
        name="rest_gradient",
    )(*map(keep, (grad_parts, weighted_high, weighted_low)))

    attended = call(
        functools.partial(attended_kernel, heads, full_width),
        out_shape=jax.ShapeDtypeStruct((groups, tokens, DH), F32),
        in_specs=[VMEM] * 3,
        out_specs=HBM,
        scratch_shapes=[
            pltpu.VMEM((groups, tokens, DH), F32),
            pltpu.SemaphoreType.DMA((groups, tokens // LOAD)),
        ],
        name="attended",
    )(keep(sums), keep(combined), gains)

    total = partner(top_grad, "seq", level_count - 1)
    parts = []
    for level in reversed(range(level_count - 1)):
        total = sum(parts, total)
        received = partner(grads[level], "seq", level)
        parts = [partner(total, "seq", level), received]
    total = call(
        finish_kernel,
        out_shape=jax.ShapeDtypeStruct((groups, DH, DH), F32),
        in_specs=[VMEM] * 3,
        out_specs=VMEM,
        name="finish",
    )(*map(keep, (total, *parts)))

    def merge(rows, count):
        rows = rows.reshape(batch_count, heads, count, DH)
        return rows.transpose(0, 2, 1, 3).reshape(batch_count, count, heads * DH)

    return merge(attended, tokens), merge(total, DH)[:, None]


def solution(mesh):
    return jax.shard_map(
        body,
        mesh=mesh,
        in_specs=(
            P(None, "seq", "head"),
            P(None, "seq", "head"),
            P(None, "seq", "head"),
            P(None, "seq", "head"),
            P(None, "head", "seq"),
            P(),
            P(None, "seq"),
            P("head"),
        ),
        out_specs=(P(None, "seq", "head"), P(None, "seq", None, "head")),
        check_vma=False,
    )
```

profile of v0, /device:TPU:0, one launch (start us, length us, event | category | flops | bytes accessed | tf_op | source)
XLA Modules:
  0.0 36.4 jit_solution(8241762345919966231)
XLA Ops:
  0.7 3.6 %state.1 = (bf16[2,2048,256]{2,1,0:T(8,128)(2,1)S(1)}, bf16[2,256,2048]{2,1,0:T(8,128)(2,1)S(1)}, bf16[2,8,128,256]{3,2,1,0:T(8,128)(2,1)S(1)}, f32[2,128,128]{2,1,0:T(8,128)S(1)}) custom-call(s32[2]{0:T(128)} %bitcast.12, f32[2,2048,128]{2,1,0:T(8,128)} %key_hbm.1, f32[2,2048,128]{2,1,0:T(8,128)} %value_hbm.1), custom_call_target="tpu_custom_call" | custom-call | tf_op jit(solution)/shard_map/state/pallas_call | solution.py:330
  4.3 0.0 copy-start
  4.3 0.6 %collective-permute-start = (f32[2,128,128]{2,1,0:T(8,128)S(1)}, f32[2,128,128]{2,1,0:T(8,128)S(1)}, u32[]{:S(2)}, u32[]{:S(2)}) collective-permute-start(f32[2,128,128]{2,1,0:T(8,128)S(1)} %get-tuple-element.35), channel_id=1, source_target_pairs={{0,8},{8,0},{16,24},{24,16},{1,9},{9,1},{17,25},{25,17},{2,10},{10... | collective-permute-start | bytes 393224 | tf_op jit(solution)/shard_map/ppermute | solution.py:299
  4.8 1.0 %collective-permute-done.refs_0_ = f32[2,128,128]{2,1,0:T(8,128)S(1)} collective-permute-done((f32[2,128,128]{2,1,0:T(8,128)S(1)}, f32[2,128,128]{2,1,0:T(8,128)S(1)}, u32[]{:S(2)}, u32[]{:S(2)}) %collective-permute-start) | collective-permute-done | bytes 131104 | tf_op jit(solution)/shard_map/ppermute | solution.py:299
  5.8 2.9 %collective-permute-start.1 = (f32[2,128,128]{2,1,0:T(8,128)S(1)}, f32[2,128,128]{2,1,0:T(8,128)S(1)}, u32[]{:S(2)}, u32[]{:S(2)}) collective-permute-start(f32[2,128,128]{2,1,0:T(8,128)S(1)} %add.15), channel_id=1, source_target_pairs={{0,16},{8,24},{16,0},{24,8},{1,17},{9,25},{17,1},{25,9},{2,18},{10... | collective-permute-start | bytes 393224 | tf_op jit(solution)/shard_map/ppermute | solution.py:299
  8.8 1.2 %token_.1 = (f32[3,2,16,128]{3,2,1,0:T(8,128)S(1)}, f32[2,128,2048]{2,1,0:T(8,128)S(1)}) custom-call(f32[3,16]{1,0:T(4,128)S(1)} %bitcast.8, s32[2,16,128]{2,1,0:T(8,128)S(1)} %bitcast.7, f32[2,2048,128]{2,1,0:T(8,128)S(1)} %copy-done.1, f32[1,128]{1,0:T(1,128)S(1)} %bitcast.9), custom_call_target="tpu_custom_call" | custom-call | tf_op jit(solution)/shard_map/token/pallas_call | solution.py:353
  10.0 3.9 %local.1 = (bf16[2,256,2048]{2,1,0:T(8,128)(2,1)S(1)}, bf16[2,256,2048]{2,1,0:T(8,128)(2,1)S(1)}, f32[2,128,2048]{2,1,0:T(8,128)S(1)}) custom-call(f32[3,2,16,128]{3,2,1,0:T(8,128)S(1)} %get-tuple-element.26.weight_ref, f32[2,2048,128]{2,1,0:T(8,128)S(1)} %copy-done, bf16[2,2048,256]{2,1,0:T(8,128)(2,1)S(1)} %get-tuple-element.28.key_ref, ...), custom_call_target="tpu_custom_call" | custom-call | tf_op jit(solution)/shard_map/local/pallas_call | solution.py:370
  13.9 1.1 %combine.1 = (f32[2,128,2048]{2,1,0:T(8,128)S(1)}, f32[2,2,16,128]{3,2,1,0:T(8,128)S(1)}) custom-call(f32[2,128,2048]{2,1,0:T(8,128)S(1)} %get-tuple-element.31.local_ref, bf16[2,256,2048]{2,1,0:T(8,128)(2,1)S(1)} %get-tuple-element.32.high_ref, bf16[2,256,2048]{2,1,0:T(8,128)(2,1)S(1)} %get-tuple-element.33.low_ref, ...), custom_call_target="tpu_custom_call" | custom-call | tf_op jit(solution)/shard_map/combine/pallas_call | solution.py:383
  15.0 1.6 %collective-permute-start.2 = (f32[2,2,16,128]{3,2,1,0:T(8,128)S(1)}, f32[2,2,16,128]{3,2,1,0:T(8,128)S(1)}, u32[]{:S(2)}, u32[]{:S(2)}) collective-permute-start(f32[2,2,16,128]{3,2,1,0:T(8,128)S(1)} %get-tuple-element.36), channel_id=1, source_target_pairs={{0,1},{1,0},{2,3},{3,2},{4,5},{5,4},{6,7},{7,6},{8,9},{9,8},{10,11... | collective-permute-start | bytes 98312 | tf_op jit(solution)/shard_map/ppermute | solution.py:304
  16.6 1.6 %collective-permute-start.3 = (f32[2,2,16,128]{3,2,1,0:T(8,128)S(1)}, f32[2,2,16,128]{3,2,1,0:T(8,128)S(1)}, u32[]{:S(2)}, u32[]{:S(2)}) collective-permute-start(f32[2,2,16,128]{3,2,1,0:T(8,128)S(1)} %get-tuple-element.36), channel_id=1, source_target_pairs={{0,2},{1,3},{2,0},{3,1},{4,6},{5,7},{6,4},{7,5},{8,10},{9,11},{10,... | collective-permute-start | bytes 98312 | tf_op jit(solution)/shard_map/ppermute | solution.py:304
  18.1 0.4 %collective-permute-start.4 = (f32[2,2,16,128]{3,2,1,0:T(8,128)S(1)}, f32[2,2,16,128]{3,2,1,0:T(8,128)S(1)}, u32[]{:S(2)}, u32[]{:S(2)}) collective-permute-start(f32[2,2,16,128]{3,2,1,0:T(8,128)S(1)} %get-tuple-element.36), channel_id=1, source_target_pairs={{0,3},{1,2},{2,1},{3,0},{4,7},{5,6},{6,5},{7,4},{8,11},{9,10},{10,... | collective-permute-start | bytes 98312 | tf_op jit(solution)/shard_map/ppermute | solution.py:304
  18.6 0.4 %collective-permute-done.2 = f32[2,2,16,128]{3,2,1,0:T(8,128)S(1)} collective-permute-done((f32[2,2,16,128]{3,2,1,0:T(8,128)S(1)}, f32[2,2,16,128]{3,2,1,0:T(8,128)S(1)}, u32[]{:S(2)}, u32[]{:S(2)}) %collective-permute-start.2) | collective-permute-done | bytes 32800 | tf_op jit(solution)/shard_map/ppermute | solution.py:304
  19.0 1.7 %collective-permute-done.3 = f32[2,2,16,128]{3,2,1,0:T(8,128)S(1)} collective-permute-done((f32[2,2,16,128]{3,2,1,0:T(8,128)S(1)}, f32[2,2,16,128]{3,2,1,0:T(8,128)S(1)}, u32[]{:S(2)}, u32[]{:S(2)}) %collective-permute-start.3) | collective-permute-done | bytes 32800 | tf_op jit(solution)/shard_map/ppermute | solution.py:304
  20.7 2.2 %collective-permute-done.4 = f32[2,2,16,128]{3,2,1,0:T(8,128)S(1)} collective-permute-done((f32[2,2,16,128]{3,2,1,0:T(8,128)S(1)}, f32[2,2,16,128]{3,2,1,0:T(8,128)S(1)}, u32[]{:S(2)}, u32[]{:S(2)}) %collective-permute-start.4) | collective-permute-done | bytes 32800 | tf_op jit(solution)/shard_map/ppermute | solution.py:304
  23.0 2.9 %collective-permute-start.5 = (f32[2,2,16,128]{3,2,1,0:T(8,128)S(1)}, f32[2,2,16,128]{3,2,1,0:T(8,128)S(1)}, u32[]{:S(2)}, u32[]{:S(2)}) collective-permute-start(f32[2,2,16,128]{3,2,1,0:T(8,128)S(1)} %add_add_fusion), channel_id=1, source_target_pairs={{0,4},{1,5},{2,6},{3,7},{4,0},{5,1},{6,2},{7,3},{8,12},{9,13},{10,... | collective-permute-start | bytes 98312 | tf_op jit(solution)/shard_map/ppermute | solution.py:304
  25.9 2.2 %collective-permute-done.5 = f32[2,2,16,128]{3,2,1,0:T(8,128)S(1)} collective-permute-done((f32[2,2,16,128]{3,2,1,0:T(8,128)S(1)}, f32[2,2,16,128]{3,2,1,0:T(8,128)S(1)}, u32[]{:S(2)}, u32[]{:S(2)}) %collective-permute-start.5) | collective-permute-done | bytes 32800 | tf_op jit(solution)/shard_map/ppermute | solution.py:304
  28.1 1.0 %top_gradient.1 = (f32[2,128,128]{2,1,0:T(8,128)S(1)}, bf16[2,256,2048]{2,1,0:T(8,128)(2,1)S(1)}) custom-call(f32[2,2,16,128]{3,2,1,0:T(8,128)S(1)} %add.19.sums_ref, f32[2,128,2048]{2,1,0:T(8,128)S(1)} %get-tuple-element.37.combined_ref, f32[2,128,2048]{2,1,0:T(8,128)S(1)} %get-tuple-element.34.scaled_ref, ...), custom_call_target="tpu_custom_call" | custom-call | tf_op jit(solution)/shard_map/top_gradient/pallas_call | solution.py:399
  29.1 0.6 %collective-permute-start.6 = (f32[2,128,128]{2,1,0:T(8,128)S(1)}, f32[2,128,128]{2,1,0:T(8,128)S(1)}, u32[]{:S(2)}, u32[]{:S(2)}) collective-permute-start(f32[2,128,128]{2,1,0:T(8,128)S(1)} %get-tuple-element.38), channel_id=1, source_target_pairs={{0,16},{8,24},{16,0},{24,8},{1,17},{9,25},{17,1},{25,9},{2,18},{10... | collective-permute-start | bytes 393224 | tf_op jit(solution)/shard_map/ppermute | solution.py:299
  29.7 0.8 %rest_gradient.1 = f32[2,128,128]{2,1,0:T(8,128)S(1)} custom-call(bf16[2,256,2048]{2,1,0:T(8,128)(2,1)S(1)} %get-tuple-element.39.parts_ref, bf16[2,256,2048]{2,1,0:T(8,128)(2,1)S(1)} %get-tuple-element.32.high_ref, bf16[2,256,2048]{2,1,0:T(8,128)(2,1)S(1)} %get-tuple-element.33.low_ref), custom_call_target="tpu_custom_call" | custom-call | tf_op jit(solution)/shard_map/rest_gradient/pallas_call | solution.py:406
  30.5 0.1 collective-permute-start.8
  30.6 3.6 %collective-permute-done.6.refs_0_ = f32[2,128,128]{2,1,0:T(8,128)S(1)} collective-permute-done((f32[2,128,128]{2,1,0:T(8,128)S(1)}, f32[2,128,128]{2,1,0:T(8,128)S(1)}, u32[]{:S(2)}, u32[]{:S(2)}) %collective-permute-start.6) | collective-permute-done | bytes 131104 | tf_op jit(solution)/shard_map/ppermute | solution.py:299
  34.2 0.0 collective-permute-start.7
  34.2 1.5 %attended.1 = f32[2,2048,128]{2,1,0:T(8,128)} custom-call(f32[2,2,16,128]{3,2,1,0:T(8,128)S(1)} %add.19.sums_ref, f32[2,128,2048]{2,1,0:T(8,128)S(1)} %get-tuple-element.37.combined_ref, f32[1,128]{1,0:T(1,128)S(1)} %bitcast.10), custom_call_target="tpu_custom_call" | custom-call | tf_op jit(solution)/shard_map/attended/pallas_call | solution.py:414
  35.7 0.7 %finish.1 = f32[2,128,128]{2,1,0:T(8,128)} custom-call(f32[2,128,128]{2,1,0:T(8,128)S(1)} %collective-permute-done.6.refs_0_, f32[2,128,128]{2,1,0:T(8,128)S(1)} %collective-permute-done.7.refs_1_, f32[2,128,128]{2,1,0:T(8,128)S(1)} %collective-permute-done.8.refs_2_), custom_call_target="tpu_custom_call" | custom-call | tf_op jit(solution)/shard_map/finish/pallas_call | solution.py:432
  (15 shorter events, 0.1 us)
Async XLA Ops:
  0.6 8.1 %copy-start.1 = (f32[2,2048,128]{2,1,0:T(8,128)S(1)}, f32[2,2048,128]{2,1,0:T(8,128)}, u32[]{:S(2)}) copy-start(f32[2,2048,128]{2,1,0:T(8,128)} %cotangent_ref) | copy-start | bytes 6291460
  0.6 8.1 %copy-start.2 = (s32[2,1,2048]{2,1,0:T(1,128)S(1)}, s32[2,1,2048]{2,1,0:T(1,128)}, u32[]{:S(2)}) copy-start(s32[2,1,2048]{2,1,0:T(1,128)} %param.12) | copy-start | bytes 49156
  0.7 8.1 %copy-start.3 = (f32[16,3]{0,1:T(4,128)S(1)}, f32[16,3]{0,1:T(4,128)}, u32[]{:S(2)}) copy-start(f32[16,3]{0,1:T(4,128)} %param.13) | copy-start | bytes 580
  0.7 8.1 %copy-start.4 = (f32[128]{0:T(128)S(1)}, f32[128]{0:T(128)}, u32[]{:S(2)}) copy-start(f32[128]{0:T(128)} %param.15) | copy-start | bytes 1540
  4.3 5.7 %copy-start = (f32[2,2048,128]{2,1,0:T(8,128)S(1)}, f32[2,2048,128]{2,1,0:T(8,128)}, u32[]{:S(2)}) copy-start(f32[2,2048,128]{2,1,0:T(8,128)} %query_ref) | copy-start | bytes 6291460
  4.3 1.5 %collective-permute-start = (f32[2,128,128]{2,1,0:T(8,128)S(1)}, f32[2,128,128]{2,1,0:T(8,128)S(1)}, u32[]{:S(2)}, u32[]{:S(2)}) collective-permute-start(f32[2,128,128]{2,1,0:T(8,128)S(1)} %get-tuple-element.35), channel_id=1, source_target_pairs={{0,8},{8,0},{16,24},{24,16},{1,9},{9,1},{17,25},{25,17},{2,10},{10... | collective-permute-start | bytes 393224 | tf_op jit(solution)/shard_map/ppermute | solution.py:299
  5.8 8.0 %collective-permute-start.1 = (f32[2,128,128]{2,1,0:T(8,128)S(1)}, f32[2,128,128]{2,1,0:T(8,128)S(1)}, u32[]{:S(2)}, u32[]{:S(2)}) collective-permute-start(f32[2,128,128]{2,1,0:T(8,128)S(1)} %add.15), channel_id=1, source_target_pairs={{0,16},{8,24},{16,0},{24,8},{1,17},{9,25},{17,1},{25,9},{2,18},{10... | collective-permute-start | bytes 393224 | tf_op jit(solution)/shard_map/ppermute | solution.py:299
  15.0 4.0 %collective-permute-start.2 = (f32[2,2,16,128]{3,2,1,0:T(8,128)S(1)}, f32[2,2,16,128]{3,2,1,0:T(8,128)S(1)}, u32[]{:S(2)}, u32[]{:S(2)}) collective-permute-start(f32[2,2,16,128]{3,2,1,0:T(8,128)S(1)} %get-tuple-element.36), channel_id=1, source_target_pairs={{0,1},{1,0},{2,3},{3,2},{4,5},{5,4},{6,7},{7,6},{8,9},{9,8},{10,11... | collective-permute-start | bytes 98312 | tf_op jit(solution)/shard_map/ppermute | solution.py:304
  16.6 4.1 %collective-permute-start.3 = (f32[2,2,16,128]{3,2,1,0:T(8,128)S(1)}, f32[2,2,16,128]{3,2,1,0:T(8,128)S(1)}, u32[]{:S(2)}, u32[]{:S(2)}) collective-permute-start(f32[2,2,16,128]{3,2,1,0:T(8,128)S(1)} %get-tuple-element.36), channel_id=1, source_target_pairs={{0,2},{1,3},{2,0},{3,1},{4,6},{5,7},{6,4},{7,5},{8,10},{9,11},{10,... | collective-permute-start | bytes 98312 | tf_op jit(solution)/shard_map/ppermute | solution.py:304
  18.1 4.8 %collective-permute-start.4 = (f32[2,2,16,128]{3,2,1,0:T(8,128)S(1)}, f32[2,2,16,128]{3,2,1,0:T(8,128)S(1)}, u32[]{:S(2)}, u32[]{:S(2)}) collective-permute-start(f32[2,2,16,128]{3,2,1,0:T(8,128)S(1)} %get-tuple-element.36), channel_id=1, source_target_pairs={{0,3},{1,2},{2,1},{3,0},{4,7},{5,6},{6,5},{7,4},{8,11},{9,10},{10,... | collective-permute-start | bytes 98312 | tf_op jit(solution)/shard_map/ppermute | solution.py:304
  23.0 5.1 %collective-permute-start.5 = (f32[2,2,16,128]{3,2,1,0:T(8,128)S(1)}, f32[2,2,16,128]{3,2,1,0:T(8,128)S(1)}, u32[]{:S(2)}, u32[]{:S(2)}) collective-permute-start(f32[2,2,16,128]{3,2,1,0:T(8,128)S(1)} %add_add_fusion), channel_id=1, source_target_pairs={{0,4},{1,5},{2,6},{3,7},{4,0},{5,1},{6,2},{7,3},{8,12},{9,13},{10,... | collective-permute-start | bytes 98312 | tf_op jit(solution)/shard_map/ppermute | solution.py:304
  29.1 5.0 %collective-permute-start.6 = (f32[2,128,128]{2,1,0:T(8,128)S(1)}, f32[2,128,128]{2,1,0:T(8,128)S(1)}, u32[]{:S(2)}, u32[]{:S(2)}) collective-permute-start(f32[2,128,128]{2,1,0:T(8,128)S(1)} %get-tuple-element.38), channel_id=1, source_target_pairs={{0,16},{8,24},{16,0},{24,8},{1,17},{9,25},{17,1},{25,9},{2,18},{10... | collective-permute-start | bytes 393224 | tf_op jit(solution)/shard_map/ppermute | solution.py:299
  30.5 5.2 %collective-permute-start.8 = (f32[2,128,128]{2,1,0:T(8,128)S(1)}, f32[2,128,128]{2,1,0:T(8,128)S(1)}, u32[]{:S(2)}, u32[]{:S(2)}) collective-permute-start(f32[2,128,128]{2,1,0:T(8,128)S(1)} %rest_gradient.1), channel_id=1, source_target_pairs={{0,8},{8,0},{16,24},{24,16},{1,9},{9,1},{17,25},{25,17},{2,10},{10... | collective-permute-start | bytes 393224 | tf_op jit(solution)/shard_map/ppermute | solution.py:299
  34.2 1.5 %collective-permute-start.7 = (f32[2,128,128]{2,1,0:T(8,128)S(1)}, f32[2,128,128]{2,1,0:T(8,128)S(1)}, u32[]{:S(2)}, u32[]{:S(2)}) collective-permute-start(f32[2,128,128]{2,1,0:T(8,128)S(1)} %collective-permute-done.6.refs_0_), channel_id=1, source_target_pairs={{0,8},{8,0},{16,24},{24,16},{1,9},{9,1},{17,25},{25,17},{2,10},{10... | collective-permute-start | bytes 393224 | tf_op jit(solution)/shard_map/ppermute | solution.py:299
where the time goes:
time: 36.6 us; the launch traced here: 36.4 us
  Pallas kernels  13.8 us (38%)
  waiting for transfers between devices  11.2 us (31%)
  starting transfers between devices  10.6 us (29%)
  between operations  0.78 us (2%)
    ppermute x4, waiting for transfers between devices, exchange(): lax.ppermute(shard, axis, [(i, i ^ mask) for i in range(size)])  6.63 us
    ppermute x4, starting transfers between devices, exchange(): lax.ppermute(shard, axis, [(i, i ^ mask) for i in range(size)])  6.43 us
    ppermute x5, waiting for transfers between devices, partner(): lax.ppermute(shard, axis, [(i, i ^ 1 << stride) for i in range(lax.axis_s...  4.57 us
    ppermute x5, starting transfers between devices, partner(): lax.ppermute(shard, axis, [(i, i ^ 1 << stride) for i in range(lax.axis_s...  4.12 us
    pallas_call x1, Pallas kernels, body(): call(local_kernel, out_shape=(resident((groups, stacked, tokens), BF16),...  3.88 us
    pallas_call x1, Pallas kernels, body(): call(functools.partial(state_kernel, heads), out_shape=(resident((groups,...  3.59 us
    pallas_call x1, Pallas kernels, body(): call(functools.partial(attended_kernel, heads, full_width), out_shape=jax...  1.52 us
    pallas_call x1, Pallas kernels, body(): call(functools.partial(token_kernel, heads), out_shape=(resident((level_c...  1.17 us
  transfers between devices with their start and end apart: 9, of which 6 were waited for; matrix products, arithmetic and copies ran while one was open for 0% of the time, Pallas kernels for 20%

commit v1 on v0

--- a/solution.py
+++ b/solution.py
@@ -10,7 +10,7 @@
 DH = 128
 LANES = 128
 CHUNK = 256
-LOAD = 512
+LOAD = 1024
 EPSILON = 1e-06
 GRANT = 8 << 20
 F32, BF16 = jnp.float32, jnp.bfloat16
@@ -38,8 +38,10 @@
         if ready is not None:
             ready(group, chunk)
         rows = pl.ds(chunk * CHUNK, CHUNK)
-        position = chunk * CHUNK + lax.broadcasted_iota(jnp.int32, (CHUNK, DH), 0)
-        live = jnp.where(position < spans[group], key_at(group, rows), 0.0)
+        live = key_at(group, rows)
+        if (chunk + 1) * CHUNK > tokens // 2:
+            position = lax.broadcasted_iota(jnp.int32, (CHUNK, DH), 0)
+            live = jnp.where(position < spans[group] - chunk * CHUNK, live, 0.0)
         key_out[group, rows, :] = jnp.concatenate(halves(live), axis=1)
         value_out[group, :, rows] = jnp.concatenate(halves(value_at(group, rows).T), axis=0)
 
@@ -219,32 +221,25 @@
     reads = lax.axis_index("seq") >> level & 1
     for group in range(groups):
         inverse, pull = factors(sums_ref, group // heads, full_width)
-        total = jnp.zeros((2 * DH, 2 * DH), F32)
         for chunk in range(tokens // CHUNK):
             rows = pl.ds(chunk * CHUNK, CHUNK)
             grad = scaled_ref[group, :, rows] * token_row(inverse, chunk) - combined_ref[
                 group, :, rows
             ] * token_row(pull, chunk)
-            both = jnp.concatenate(halves(grad), axis=0)
-            parts_out[group, :, rows] = both
-            weighted = jnp.concatenate([high_ref[group, top, rows], low_ref[group, top, rows]], 0)
-            total = total + dot(both, weighted, NT)
+            parts_out[group, :, rows] = jnp.concatenate(halves(grad), axis=0)
+        weighted = jnp.concatenate([high_ref[group, top, :], low_ref[group, top, :]], 0)
+        total = dot(parts_out[group], weighted, NT)
         grad_out[group] = jnp.where(reads == 1, fold(total), 0.0)
 
 
 def rest_gradient_kernel(parts_ref, high_ref, low_ref, *grad_outs):
-    groups, _, tokens = parts_ref.shape
+    groups, _, _ = parts_ref.shape
     for level, grad_out in enumerate(grad_outs):
         spot = pl.ds(level * DH, DH)
         reads = lax.axis_index("seq") >> level & 1
         for group in range(groups):
-            total = jnp.zeros((2 * DH, 2 * DH), F32)
-            for chunk in range(tokens // CHUNK):
-                rows = pl.ds(chunk * CHUNK, CHUNK)
-                weighted = jnp.concatenate(
-                    [high_ref[group, spot, rows], low_ref[group, spot, rows]], 0
-                )
-                total = total + dot(parts_ref[group, :, rows], weighted, NT)
+            weighted = jnp.concatenate([high_ref[group, spot, :], low_ref[group, spot, :]], 0)
+            total = dot(parts_ref[group], weighted, NT)
             grad_out[group] = jnp.where(reads == 1, fold(total), 0.0)
 
 
@@ -392,9 +387,10 @@
     )(*map(keep, (local_sum, weighted_high, weighted_low, scaled, *buckets)))
 
     head_bits = lax.axis_size("head").bit_length() - 1
-    sums = exchange(sums, "head", range(1, 1 << min(2, head_bits)))
-    for level in range(2, head_bits):
-        sums = exchange(sums, "head", (1 << level,))
+    rounds = [(1, 3, 2)[: (1 << min(2, head_bits)) - 1]]
+    rounds += [(1 << level,) for level in range(2, head_bits)]
+    for masks in rounds:
+        sums = exchange(sums, "head", masks)
 
     top_grad, grad_parts = call(
         functools.partial(top_gradient_kernel, heads, full_width),

time: 36.6 us -> 34.7 us (0.948)
  waiting for transfers between devices: 11.2 us -> 10.2 us
  Pallas kernels: 13.8 us -> 13.1 us
    ppermute x4, waiting for transfers between devices: 6.63 us -> 5.69 us  [exchange(): lax.ppermute(shard, axis, [(i, i ^ mask) for i in range(size)])]
    pallas_call x1, Pallas kernels: 3.59 us -> 2.94 us  [body(): call(functools.partial(state_kernel, heads), out_shape=(resident((groups,...]
  transfers between devices with their start and end apart: 9 -> 9, of which waited for: 6 -> 6; matrix products, arithmetic and copies ran while one was open for 0% -> 0% of each run, Pallas kernels for 20% -> 21%
where the time goes in v1:
time: 34.7 us; the launch traced here: 34.5 us
  Pallas kernels  13.1 us (38%)
  starting transfers between devices  10.3 us (30%)
  waiting for transfers between devices  10.2 us (29%)
  between operations  0.78 us (2%)
    ppermute x4, starting transfers between devices, exchange(): lax.ppermute(shard, axis, [(i, i ^ mask) for i in range(size)])  6.21 us
    ppermute x4, waiting for transfers between devices, exchange(): lax.ppermute(shard, axis, [(i, i ^ mask) for i in range(size)])  5.69 us
    ppermute x5, waiting for transfers between devices, partner(): lax.ppermute(shard, axis, [(i, i ^ 1 << stride) for i in range(lax.axis_s...  4.56 us
    ppermute x5, starting transfers between devices, partner(): lax.ppermute(shard, axis, [(i, i ^ 1 << stride) for i in range(lax.axis_s...  4.13 us
    pallas_call x1, Pallas kernels, body(): call(local_kernel, out_shape=(resident((groups, stacked, tokens), BF16),...  3.88 us
    pallas_call x1, Pallas kernels, body(): call(functools.partial(state_kernel, heads), out_shape=(resident((groups,...  2.94 us
    pallas_call x1, Pallas kernels, body(): call(functools.partial(attended_kernel, heads, full_width), out_shape=jax...  1.56 us
    pallas_call x1, Pallas kernels, body(): call(functools.partial(token_kernel, heads), out_shape=(resident((level_c...  1.17 us
  transfers between devices with their start and end apart: 9, of which 6 were waited for; matrix products, arithmetic and copies ran while one was open for 0% of the time, Pallas kernels for 21%

profile of v1, /device:TPU:0, one launch (start us, length us, event | category | flops | bytes accessed | tf_op | source)
XLA Modules:
  0.0 34.5 jit_solution(18250642618717677985)
XLA Ops:
  0.7 2.9 %state.1 = (bf16[2,2048,256]{2,1,0:T(8,128)(2,1)S(1)}, bf16[2,256,2048]{2,1,0:T(8,128)(2,1)S(1)}, bf16[2,8,128,256]{3,2,1,0:T(8,128)(2,1)S(1)}, f32[2,128,128]{2,1,0:T(8,128)S(1)}) custom-call(s32[2]{0:T(128)} %bitcast.12, f32[2,2048,128]{2,1,0:T(8,128)} %key_hbm.1, f32[2,2048,128]{2,1,0:T(8,128)} %value_hbm.1), custom_call_target="tpu_custom_call" | custom-call | tf_op jit(solution)/shard_map/state/pallas_call | solution.py:325
  3.6 0.0 copy-start
  3.6 0.6 %collective-permute-start = (f32[2,128,128]{2,1,0:T(8,128)S(1)}, f32[2,128,128]{2,1,0:T(8,128)S(1)}, u32[]{:S(2)}, u32[]{:S(2)}) collective-permute-start(f32[2,128,128]{2,1,0:T(8,128)S(1)} %get-tuple-element.35), channel_id=1, source_target_pairs={{0,8},{8,0},{16,24},{24,16},{1,9},{9,1},{17,25},{25,17},{2,10},{10... | collective-permute-start | bytes 393224 | tf_op jit(solution)/shard_map/ppermute | solution.py:294
  4.2 1.0 %collective-permute-done.refs_0_ = f32[2,128,128]{2,1,0:T(8,128)S(1)} collective-permute-done((f32[2,128,128]{2,1,0:T(8,128)S(1)}, f32[2,128,128]{2,1,0:T(8,128)S(1)}, u32[]{:S(2)}, u32[]{:S(2)}) %collective-permute-start) | collective-permute-done | bytes 131104 | tf_op jit(solution)/shard_map/ppermute | solution.py:294
  5.2 2.9 %collective-permute-start.1 = (f32[2,128,128]{2,1,0:T(8,128)S(1)}, f32[2,128,128]{2,1,0:T(8,128)S(1)}, u32[]{:S(2)}, u32[]{:S(2)}) collective-permute-start(f32[2,128,128]{2,1,0:T(8,128)S(1)} %add.15), channel_id=1, source_target_pairs={{0,16},{8,24},{16,0},{24,8},{1,17},{9,25},{17,1},{25,9},{2,18},{10... | collective-permute-start | bytes 393224 | tf_op jit(solution)/shard_map/ppermute | solution.py:294
  8.1 1.2 %token_.1 = (f32[3,2,16,128]{3,2,1,0:T(8,128)S(1)}, f32[2,128,2048]{2,1,0:T(8,128)S(1)}) custom-call(f32[3,16]{1,0:T(4,128)S(1)} %bitcast.8, s32[2,16,128]{2,1,0:T(8,128)S(1)} %bitcast.7, f32[2,2048,128]{2,1,0:T(8,128)S(1)} %copy-done.1, f32[1,128]{1,0:T(1,128)S(1)} %bitcast.9), custom_call_target="tpu_custom_call" | custom-call | tf_op jit(solution)/shard_map/token/pallas_call | solution.py:348
  9.3 3.9 %local.1 = (bf16[2,256,2048]{2,1,0:T(8,128)(2,1)S(1)}, bf16[2,256,2048]{2,1,0:T(8,128)(2,1)S(1)}, f32[2,128,2048]{2,1,0:T(8,128)S(1)}) custom-call(f32[3,2,16,128]{3,2,1,0:T(8,128)S(1)} %get-tuple-element.26.weight_ref, f32[2,2048,128]{2,1,0:T(8,128)S(1)} %copy-done, bf16[2,2048,256]{2,1,0:T(8,128)(2,1)S(1)} %get-tuple-element.28.key_ref, ...), custom_call_target="tpu_custom_call" | custom-call | tf_op jit(solution)/shard_map/local/pallas_call | solution.py:365
  13.2 1.1 %combine.1 = (f32[2,128,2048]{2,1,0:T(8,128)S(1)}, f32[2,2,16,128]{3,2,1,0:T(8,128)S(1)}) custom-call(f32[2,128,2048]{2,1,0:T(8,128)S(1)} %get-tuple-element.31.local_ref, bf16[2,256,2048]{2,1,0:T(8,128)(2,1)S(1)} %get-tuple-element.32.high_ref, bf16[2,256,2048]{2,1,0:T(8,128)(2,1)S(1)} %get-tuple-element.33.low_ref, ...), custom_call_target="tpu_custom_call" | custom-call | tf_op jit(solution)/shard_map/combine/pallas_call | solution.py:378
  14.4 1.6 %collective-permute-start.2 = (f32[2,2,16,128]{3,2,1,0:T(8,128)S(1)}, f32[2,2,16,128]{3,2,1,0:T(8,128)S(1)}, u32[]{:S(2)}, u32[]{:S(2)}) collective-permute-start(f32[2,2,16,128]{3,2,1,0:T(8,128)S(1)} %get-tuple-element.36), channel_id=1, source_target_pairs={{0,1},{1,0},{2,3},{3,2},{4,5},{5,4},{6,7},{7,6},{8,9},{9,8},{10,11... | collective-permute-start | bytes 98312 | tf_op jit(solution)/shard_map/ppermute | solution.py:299
  15.9 1.5 %collective-permute-start.3 = (f32[2,2,16,128]{3,2,1,0:T(8,128)S(1)}, f32[2,2,16,128]{3,2,1,0:T(8,128)S(1)}, u32[]{:S(2)}, u32[]{:S(2)}) collective-permute-start(f32[2,2,16,128]{3,2,1,0:T(8,128)S(1)} %get-tuple-element.36), channel_id=1, source_target_pairs={{0,3},{1,2},{2,1},{3,0},{4,7},{5,6},{6,5},{7,4},{8,11},{9,10},{10,... | collective-permute-start | bytes 98312 | tf_op jit(solution)/shard_map/ppermute | solution.py:299
  17.5 0.4 %collective-permute-start.4 = (f32[2,2,16,128]{3,2,1,0:T(8,128)S(1)}, f32[2,2,16,128]{3,2,1,0:T(8,128)S(1)}, u32[]{:S(2)}, u32[]{:S(2)}) collective-permute-start(f32[2,2,16,128]{3,2,1,0:T(8,128)S(1)} %get-tuple-element.36), channel_id=1, source_target_pairs={{0,2},{1,3},{2,0},{3,1},{4,6},{5,7},{6,4},{7,5},{8,10},{9,11},{10,... | collective-permute-start | bytes 98312 | tf_op jit(solution)/shard_map/ppermute | solution.py:299
  17.9 0.4 %collective-permute-done.2 = f32[2,2,16,128]{3,2,1,0:T(8,128)S(1)} collective-permute-done((f32[2,2,16,128]{3,2,1,0:T(8,128)S(1)}, f32[2,2,16,128]{3,2,1,0:T(8,128)S(1)}, u32[]{:S(2)}, u32[]{:S(2)}) %collective-permute-start.2) | collective-permute-done | bytes 32800 | tf_op jit(solution)/shard_map/ppermute | solution.py:299
  18.3 2.7 %collective-permute-done.3 = f32[2,2,16,128]{3,2,1,0:T(8,128)S(1)} collective-permute-done((f32[2,2,16,128]{3,2,1,0:T(8,128)S(1)}, f32[2,2,16,128]{3,2,1,0:T(8,128)S(1)}, u32[]{:S(2)}, u32[]{:S(2)}) %collective-permute-start.3) | collective-permute-done | bytes 32800 | tf_op jit(solution)/shard_map/ppermute | solution.py:299
  21.0 0.4 %collective-permute-done.4 = f32[2,2,16,128]{3,2,1,0:T(8,128)S(1)} collective-permute-done((f32[2,2,16,128]{3,2,1,0:T(8,128)S(1)}, f32[2,2,16,128]{3,2,1,0:T(8,128)S(1)}, u32[]{:S(2)}, u32[]{:S(2)}) %collective-permute-start.4) | collective-permute-done | bytes 32800 | tf_op jit(solution)/shard_map/ppermute | solution.py:299
  21.4 2.7 %collective-permute-start.5 = (f32[2,2,16,128]{3,2,1,0:T(8,128)S(1)}, f32[2,2,16,128]{3,2,1,0:T(8,128)S(1)}, u32[]{:S(2)}, u32[]{:S(2)}) collective-permute-start(f32[2,2,16,128]{3,2,1,0:T(8,128)S(1)} %add_add_fusion), channel_id=1, source_target_pairs={{0,4},{1,5},{2,6},{3,7},{4,0},{5,1},{6,2},{7,3},{8,12},{9,13},{10,... | collective-permute-start | bytes 98312 | tf_op jit(solution)/shard_map/ppermute | solution.py:299
  24.1 2.2 %collective-permute-done.5 = f32[2,2,16,128]{3,2,1,0:T(8,128)S(1)} collective-permute-done((f32[2,2,16,128]{3,2,1,0:T(8,128)S(1)}, f32[2,2,16,128]{3,2,1,0:T(8,128)S(1)}, u32[]{:S(2)}, u32[]{:S(2)}) %collective-permute-start.5) | collective-permute-done | bytes 32800 | tf_op jit(solution)/shard_map/ppermute | solution.py:299
  26.3 0.9 %top_gradient.1 = (f32[2,128,128]{2,1,0:T(8,128)S(1)}, bf16[2,256,2048]{2,1,0:T(8,128)(2,1)S(1)}) custom-call(f32[2,2,16,128]{3,2,1,0:T(8,128)S(1)} %add.19.sums_ref, f32[2,128,2048]{2,1,0:T(8,128)S(1)} %get-tuple-element.37.combined_ref, f32[2,128,2048]{2,1,0:T(8,128)S(1)} %get-tuple-element.34.scaled_ref, ...), custom_call_target="tpu_custom_call" | custom-call | tf_op jit(solution)/shard_map/top_gradient/pallas_call | solution.py:395
  27.2 0.6 %collective-permute-start.6 = (f32[2,128,128]{2,1,0:T(8,128)S(1)}, f32[2,128,128]{2,1,0:T(8,128)S(1)}, u32[]{:S(2)}, u32[]{:S(2)}) collective-permute-start(f32[2,128,128]{2,1,0:T(8,128)S(1)} %get-tuple-element.38), channel_id=1, source_target_pairs={{0,16},{8,24},{16,0},{24,8},{1,17},{9,25},{17,1},{25,9},{2,18},{10... | collective-permute-start | bytes 393224 | tf_op jit(solution)/shard_map/ppermute | solution.py:294
  27.8 0.8 %rest_gradient.1 = f32[2,128,128]{2,1,0:T(8,128)S(1)} custom-call(bf16[2,256,2048]{2,1,0:T(8,128)(2,1)S(1)} %get-tuple-element.39.parts_ref, bf16[2,256,2048]{2,1,0:T(8,128)(2,1)S(1)} %get-tuple-element.32.high_ref, bf16[2,256,2048]{2,1,0:T(8,128)(2,1)S(1)} %get-tuple-element.33.low_ref), custom_call_target="tpu_custom_call" | custom-call | tf_op jit(solution)/shard_map/rest_gradient/pallas_call | solution.py:402
  28.6 0.1 collective-permute-start.8
  28.7 3.6 %collective-permute-done.6.refs_0_ = f32[2,128,128]{2,1,0:T(8,128)S(1)} collective-permute-done((f32[2,128,128]{2,1,0:T(8,128)S(1)}, f32[2,128,128]{2,1,0:T(8,128)S(1)}, u32[]{:S(2)}, u32[]{:S(2)}) %collective-permute-start.6) | collective-permute-done | bytes 131104 | tf_op jit(solution)/shard_map/ppermute | solution.py:294
  32.2 1.6 %attended.1 = f32[2,2048,128]{2,1,0:T(8,128)} custom-call(f32[2,2,16,128]{3,2,1,0:T(8,128)S(1)} %add.19.sums_ref, f32[2,128,2048]{2,1,0:T(8,128)S(1)} %get-tuple-element.37.combined_ref, f32[1,128]{1,0:T(1,128)S(1)} %bitcast.10), custom_call_target="tpu_custom_call" | custom-call | tf_op jit(solution)/shard_map/attended/pallas_call | solution.py:410
  33.8 0.0 collective-permute-done.8.refs_2_
  33.8 0.7 %finish.1 = f32[2,128,128]{2,1,0:T(8,128)} custom-call(f32[2,128,128]{2,1,0:T(8,128)S(1)} %collective-permute-done.6.refs_0_, f32[2,128,128]{2,1,0:T(8,128)S(1)} %collective-permute-done.7.refs_1_, f32[2,128,128]{2,1,0:T(8,128)S(1)} %collective-permute-done.8.refs_2_), custom_call_target="tpu_custom_call" | custom-call | tf_op jit(solution)/shard_map/finish/pallas_call | solution.py:428
  (15 shorter events, 0.1 us)
Async XLA Ops:
  0.6 7.5 %copy-start.1 = (f32[2,2048,128]{2,1,0:T(8,128)S(1)}, f32[2,2048,128]{2,1,0:T(8,128)}, u32[]{:S(2)}) copy-start(f32[2,2048,128]{2,1,0:T(8,128)} %cotangent_ref) | copy-start | bytes 6291460
  0.6 7.5 %copy-start.2 = (s32[2,1,2048]{2,1,0:T(1,128)S(1)}, s32[2,1,2048]{2,1,0:T(1,128)}, u32[]{:S(2)}) copy-start(s32[2,1,2048]{2,1,0:T(1,128)} %param.12) | copy-start | bytes 49156
  0.7 7.5 %copy-start.3 = (f32[16,3]{0,1:T(4,128)S(1)}, f32[16,3]{0,1:T(4,128)}, u32[]{:S(2)}) copy-start(f32[16,3]{0,1:T(4,128)} %param.13) | copy-start | bytes 580
  0.7 7.5 %copy-start.4 = (f32[128]{0:T(128)S(1)}, f32[128]{0:T(128)}, u32[]{:S(2)}) copy-start(f32[128]{0:T(128)} %param.15) | copy-start | bytes 1540
  3.6 5.7 %copy-start = (f32[2,2048,128]{2,1,0:T(8,128)S(1)}, f32[2,2048,128]{2,1,0:T(8,128)}, u32[]{:S(2)}) copy-start(f32[2,2048,128]{2,1,0:T(8,128)} %query_ref) | copy-start | bytes 6291460
  3.6 1.5 %collective-permute-start = (f32[2,128,128]{2,1,0:T(8,128)S(1)}, f32[2,128,128]{2,1,0:T(8,128)S(1)}, u32[]{:S(2)}, u32[]{:S(2)}) collective-permute-start(f32[2,128,128]{2,1,0:T(8,128)S(1)} %get-tuple-element.35), channel_id=1, source_target_pairs={{0,8},{8,0},{16,24},{24,16},{1,9},{9,1},{17,25},{25,17},{2,10},{10... | collective-permute-start | bytes 393224 | tf_op jit(solution)/shard_map/ppermute | solution.py:294
  5.2 8.0 %collective-permute-start.1 = (f32[2,128,128]{2,1,0:T(8,128)S(1)}, f32[2,128,128]{2,1,0:T(8,128)S(1)}, u32[]{:S(2)}, u32[]{:S(2)}) collective-permute-start(f32[2,128,128]{2,1,0:T(8,128)S(1)} %add.15), channel_id=1, source_target_pairs={{0,16},{8,24},{16,0},{24,8},{1,17},{9,25},{17,1},{25,9},{2,18},{10... | collective-permute-start | bytes 393224 | tf_op jit(solution)/shard_map/ppermute | solution.py:294
  14.4 4.0 %collective-permute-start.2 = (f32[2,2,16,128]{3,2,1,0:T(8,128)S(1)}, f32[2,2,16,128]{3,2,1,0:T(8,128)S(1)}, u32[]{:S(2)}, u32[]{:S(2)}) collective-permute-start(f32[2,2,16,128]{3,2,1,0:T(8,128)S(1)} %get-tuple-element.36), channel_id=1, source_target_pairs={{0,1},{1,0},{2,3},{3,2},{4,5},{5,4},{6,7},{7,6},{8,9},{9,8},{10,11... | collective-permute-start | bytes 98312 | tf_op jit(solution)/shard_map/ppermute | solution.py:299
  15.9 5.1 %collective-permute-start.3 = (f32[2,2,16,128]{3,2,1,0:T(8,128)S(1)}, f32[2,2,16,128]{3,2,1,0:T(8,128)S(1)}, u32[]{:S(2)}, u32[]{:S(2)}) collective-permute-start(f32[2,2,16,128]{3,2,1,0:T(8,128)S(1)} %get-tuple-element.36), channel_id=1, source_target_pairs={{0,3},{1,2},{2,1},{3,0},{4,7},{5,6},{6,5},{7,4},{8,11},{9,10},{10,... | collective-permute-start | bytes 98312 | tf_op jit(solution)/shard_map/ppermute | solution.py:299
  17.5 3.9 %collective-permute-start.4 = (f32[2,2,16,128]{3,2,1,0:T(8,128)S(1)}, f32[2,2,16,128]{3,2,1,0:T(8,128)S(1)}, u32[]{:S(2)}, u32[]{:S(2)}) collective-permute-start(f32[2,2,16,128]{3,2,1,0:T(8,128)S(1)} %get-tuple-element.36), channel_id=1, source_target_pairs={{0,2},{1,3},{2,0},{3,1},{4,6},{5,7},{6,4},{7,5},{8,10},{9,11},{10,... | collective-permute-start | bytes 98312 | tf_op jit(solution)/shard_map/ppermute | solution.py:299
  21.4 4.9 %collective-permute-start.5 = (f32[2,2,16,128]{3,2,1,0:T(8,128)S(1)}, f32[2,2,16,128]{3,2,1,0:T(8,128)S(1)}, u32[]{:S(2)}, u32[]{:S(2)}) collective-permute-start(f32[2,2,16,128]{3,2,1,0:T(8,128)S(1)} %add_add_fusion), channel_id=1, source_target_pairs={{0,4},{1,5},{2,6},{3,7},{4,0},{5,1},{6,2},{7,3},{8,12},{9,13},{10,... | collective-permute-start | bytes 98312 | tf_op jit(solution)/shard_map/ppermute | solution.py:299
  27.2 5.0 %collective-permute-start.6 = (f32[2,128,128]{2,1,0:T(8,128)S(1)}, f32[2,128,128]{2,1,0:T(8,128)S(1)}, u32[]{:S(2)}, u32[]{:S(2)}) collective-permute-start(f32[2,128,128]{2,1,0:T(8,128)S(1)} %get-tuple-element.38), channel_id=1, source_target_pairs={{0,16},{8,24},{16,0},{24,8},{1,17},{9,25},{17,1},{25,9},{2,18},{10... | collective-permute-start | bytes 393224 | tf_op jit(solution)/shard_map/ppermute | solution.py:294
  28.6 5.2 %collective-permute-start.8 = (f32[2,128,128]{2,1,0:T(8,128)S(1)}, f32[2,128,128]{2,1,0:T(8,128)S(1)}, u32[]{:S(2)}, u32[]{:S(2)}) collective-permute-start(f32[2,128,128]{2,1,0:T(8,128)S(1)} %rest_gradient.1), channel_id=1, source_target_pairs={{0,8},{8,0},{16,24},{24,16},{1,9},{9,1},{17,25},{25,17},{2,10},{10... | collective-permute-start | bytes 393224 | tf_op jit(solution)/shard_map/ppermute | solution.py:294
  32.2 1.6 %collective-permute-start.7 = (f32[2,128,128]{2,1,0:T(8,128)S(1)}, f32[2,128,128]{2,1,0:T(8,128)S(1)}, u32[]{:S(2)}, u32[]{:S(2)}) collective-permute-start(f32[2,128,128]{2,1,0:T(8,128)S(1)} %collective-permute-done.6.refs_0_), channel_id=1, source_target_pairs={{0,8},{8,0},{16,24},{24,16},{1,9},{9,1},{17,25},{25,17},{2,10},{10... | collective-permute-start | bytes 393224 | tf_op jit(solution)/shard_map/ppermute | solution.py:294

commit v2 on v1

--- a/solution.py
+++ b/solution.py
@@ -52,7 +52,7 @@
             prepare(*spots[index + 1])
         rows = pl.ds(chunk * CHUNK, CHUNK)
         total = jnp.zeros((DH, DH), F32) if chunk == 0 else total
-        prefix_out[group, chunk] = jnp.concatenate(halves(total), axis=1)
+        prefix_out[group, chunk] = total
         square = dot(value_out[group, :, rows], key_out[group, rows, :])
         square = square[:DH] + square[DH:]
         total = total + (square[:, :DH] + square[:, DH:])
@@ -60,11 +60,29 @@
             state_out[group] = total
 
 
-def state_kernel(heads, span_hbm, key_hbm, value_hbm, *refs):
-    *outs, span_ref, key_ref, value_ref, span_sem, sems = refs
+def level_weights(table_ref, selector_ref, weight_out):
+    levels, choices = table_ref.shape
+    for group in range(selector_ref.shape[0]):
+        selector = selector_ref[group]
+        for level in range(levels):
+            weight = jnp.zeros(selector.shape, F32)
+            for choice in range(choices):
+                weight = jnp.where(selector == choice, table_ref[level, choice], weight)
+            weight_out[level, group] = weight
+
+
+def state_kernel(heads, span_hbm, table_hbm, selector_hbm, key_hbm, value_hbm, *refs):
+    *outs, weight_out = refs[:5]
+    span_ref, table_ref, selector_ref, key_ref, value_ref, small_sems, sems = refs[5:]
     groups, tokens, _ = key_ref.shape
-    span_copy = pltpu.make_async_copy(span_hbm, span_ref, span_sem)
-    span_copy.start()
+    small = [
+        pltpu.make_async_copy(source, target, small_sems.at[index])
+        for index, (source, target) in enumerate(
+            ((span_hbm, span_ref), (table_hbm, table_ref), (selector_hbm, selector_ref))
+        )
+    ]
+    for copy in small:
+        copy.start()
     loads = {}
     for group in range(groups):
         for load in range(tokens // LOAD):
@@ -79,12 +97,16 @@
             ]
             for copy in loads[group, load]:
                 copy.start()
-    span_copy.wait()
+    small[0].wait()
 
     def ready(group, chunk):
         if chunk * CHUNK % LOAD == 0:
             for copy in loads[group, chunk * CHUNK // LOAD]:
                 copy.wait()
+        if group == 0 and (chunk + 1) * CHUNK == tokens:
+            for copy in small[1:]:
+                copy.wait()
+            level_weights(table_ref, selector_ref, weight_out)
 
     chunk_states(
         groups,
@@ -95,23 +117,6 @@
         outs,
         ready,
     )
-
-
-def token_kernel(heads, table_ref, selector_ref, cotangent_ref, gain_ref, weight_out, scaled_out):
-    groups, tokens, _ = cotangent_ref.shape
-    levels, choices = table_ref.shape
-    for group in range(groups):
-        gain = gain_ref[pl.ds(group % heads, 1), :]
-        for chunk in range(tokens // CHUNK):
-            rows = pl.ds(chunk * CHUNK, CHUNK)
-            scaled_out[group, :, rows] = (cotangent_ref[group, rows, :] * gain).T
-    for group in range(groups):
-        selector = selector_ref[group]
-        for level in range(levels):
-            weight = jnp.zeros(selector.shape, F32)
-            for choice in range(choices):
-                weight = jnp.where(selector == choice, table_ref[level, choice], weight)
-            weight_out[level, group] = weight
 
 
 def causal_halves(scores, ahead):
@@ -128,6 +133,15 @@
     return [jnp.concatenate(parts, axis=0) for parts in zip(*strips)]
 
 
+def scale_kernel(heads, cotangent_ref, gain_ref, scaled_out):
+    groups, tokens, _ = cotangent_ref.shape
+    for group in range(groups):
+        gain = gain_ref[pl.ds(group % heads, 1), :]
+        for chunk in range(tokens // CHUNK):
+            rows = pl.ds(chunk * CHUNK, CHUNK)
+            scaled_out[group, :, rows] = (cotangent_ref[group, rows, :] * gain).T
+
+
 def local_kernel(weight_ref, query_ref, key_ref, value_ref, prefix_ref, *refs):
     high_out, low_out, local_out, high_own, low_own = refs
     groups, tokens, _ = query_ref.shape
@@ -155,7 +169,8 @@
             prepare(index + 1)
         rows = pl.ds(chunk * CHUNK, CHUNK)
         high, low = high_own[index % 2], low_own[index % 2]
-        left = jnp.concatenate([key_ref[group, rows, :], prefix_ref[group, chunk]], axis=0)
+        prefix = jnp.concatenate(halves(prefix_ref[group, chunk]), axis=1)
+        left = jnp.concatenate([key_ref[group, rows, :], prefix], axis=0)
         mixed = dot(left, jnp.concatenate([high, high], axis=0)) + dot(left[:, :DH], low)
         scores_high, scores_low = causal_halves(mixed[:CHUNK], ahead)
         values = value_ref[group, :, rows]
@@ -322,45 +337,43 @@
         pl.pallas_call, compiler_params=pltpu.CompilerParams(vmem_limit_bytes=GRANT)
     )
 
-    key_parts, value_parts, prefixes, state = call(
+    key_parts, value_parts, prefixes, state, weights = call(
         functools.partial(state_kernel, heads),
         out_shape=(
             resident((groups, tokens, 2 * DH), BF16),
             resident((groups, 2 * DH, tokens), BF16),
-            resident((groups, chunks, DH, 2 * DH), BF16),
+            resident((groups, chunks, DH, DH)),
             resident((groups, DH, DH)),
+            resident((level_count + 1, groups, tokens // LANES, LANES)),
         ),
-        in_specs=[HBM] * 3,
-        out_specs=(VMEM,) * 4,
+        in_specs=[HBM] * 5,
+        out_specs=(VMEM,) * 5,
         scratch_shapes=[
             pltpu.SMEM((batch_count,), jnp.int32),
+            pltpu.SMEM(level_table.shape[::-1], F32),
+            pltpu.VMEM(selectors.shape, jnp.int32),
             pltpu.VMEM((groups, tokens, DH), F32),
             pltpu.VMEM((groups, tokens, DH), F32),
-            pltpu.SemaphoreType.DMA(()),
+            pltpu.SemaphoreType.DMA((3,)),
             pltpu.SemaphoreType.DMA((2, groups, tokens // LOAD)),
         ],
         name="state",
-    )(*map(leave, (span_length.reshape(batch_count), keys, values)))
-    state, queries, cotangents, gains, selectors, level_table = lax.optimization_barrier(
-        (state, queries, cotangents, gains, selectors, level_table)
-    )
-
-    weights, scaled = call(
-        functools.partial(token_kernel, heads),
-        out_shape=(
-            resident((level_count + 1, groups, tokens // LANES, LANES)),
-            resident((groups, DH, tokens)),
-        ),
-        in_specs=[SMEM] + [VMEM] * 3,
-        out_specs=(VMEM,) * 2,
-        name="token",
-    )(level_table.T, selectors, cotangents, gains)
+    )(
+        *map(
+            leave,
+            (span_length.reshape(batch_count), level_table.T, selectors, keys, values),
+        )
+    )
+    state, queries, cotangents, gains = lax.optimization_barrier(
+        (state, queries, cotangents, gains)
+    )
 
     buckets = []
-    pending = state
-    for level in range(level_count):
-        buckets.append(partner(pending, "seq", level))
-        pending = pending + buckets[-1]
+    for level in reversed(range(level_count)):
+        bucket = partner(state, "seq", level)
+        for lower in reversed(range(level)):
+            bucket = bucket + partner(bucket, "seq", lower)
+        buckets.insert(0, bucket)
 
     weighted_high, weighted_low, local_sum = call(
         local_kernel,
@@ -374,6 +387,14 @@
         scratch_shapes=[pltpu.VMEM((2, DH, CHUNK), BF16)] * 2,
         name="local",
     )(*map(keep, (weights, queries, key_parts, value_parts, prefixes)))
+
+    scaled = call(
+        functools.partial(scale_kernel, heads),
+        out_shape=resident((groups, DH, tokens)),
+        in_specs=[VMEM] * 2,
+        out_specs=VMEM,
+        name="scale",
+    )(cotangents, gains)
 
     combined, sums = call(
         functools.partial(combine_kernel, heads),

time: 34.7 us -> 37.1 us (1.069)
  waiting for transfers between devices: 10.2 us -> 12 us
  starting transfers between devices: 10.3 us -> 11.4 us
  Pallas kernels: 13.1 us -> 12.7 us
    ppermute x5 -> x6, waiting for transfers between devices: 4.56 us -> 6.06 us  [partner(): lax.ppermute(shard, axis, [(i, i ^ 1 << stride) for i in range(lax.axis_s...]
    ppermute x5 -> x6, starting transfers between devices: 4.13 us -> 5.23 us  [partner(): lax.ppermute(shard, axis, [(i, i ^ 1 << stride) for i in range(lax.axis_s...]
    pallas_call x1, Pallas kernels: 1.17 us -> 0.6 us  [body(): call(functools.partial(scale_kernel, heads), out_shape=resident((groups,...]
  transfers between devices with their start and end apart: 9 -> 10, of which waited for: 6 -> 6; matrix products, arithmetic and copies ran while one was open for 0% -> 0% of each run, Pallas kernels for 21% -> 19%
where the time goes in v2:
time: 37.1 us; the launch traced here: 37 us
  Pallas kernels  12.7 us (34%)
  waiting for transfers between devices  12 us (32%)
  starting transfers between devices  11.4 us (31%)
  between operations  0.78 us (2%)
    ppermute x4, starting transfers between devices, exchange(): lax.ppermute(shard, axis, [(i, i ^ mask) for i in range(size)])  6.2 us
    ppermute x6, waiting for transfers between devices, partner(): lax.ppermute(shard, axis, [(i, i ^ 1 << stride) for i in range(lax.axis_s...  6.06 us
    ppermute x4, waiting for transfers between devices, exchange(): lax.ppermute(shard, axis, [(i, i ^ mask) for i in range(size)])  5.91 us
    ppermute x6, starting transfers between devices, partner(): lax.ppermute(shard, axis, [(i, i ^ 1 << stride) for i in range(lax.axis_s...  5.23 us
    pallas_call x1, Pallas kernels, body(): call(local_kernel, out_shape=(resident((groups, stacked, tokens), BF16),...  3.89 us
    pallas_call x1, Pallas kernels, body(): call(functools.partial(state_kernel, heads), out_shape=(resident((groups,...  3.18 us
    pallas_call x1, Pallas kernels, body(): call(functools.partial(attended_kernel, heads, full_width), out_shape=jax...  1.56 us
    pallas_call x1, Pallas kernels, body(): call(functools.partial(combine_kernel, heads), out_shape=(resident((group...  1.12 us
  transfers between devices with their start and end apart: 10, of which 6 were waited for; matrix products, arithmetic and copies ran while one was open for 0% of the time, Pallas kernels for 19%

profile of v2, /device:TPU:0, one launch (start us, length us, event | category | flops | bytes accessed | tf_op | source)
XLA Modules:
  0.0 37.0 jit_solution(8324063999546244856)
XLA Ops:
  0.7 3.2 %state.1 = (bf16[2,2048,256]{2,1,0:T(8,128)(2,1)S(1)}, bf16[2,256,2048]{2,1,0:T(8,128)(2,1)S(1)}, f32[2,8,128,128]{3,2,1,0:T(8,128)S(1)}, f32[2,128,128]{2,1,0:T(8,128)S(1)}, f32[3,2,16,128]{3,2,1,0:T(8,128)S(1)}) custom-call(s32[2]{0:T(128)} %bitcast.12, f32[3,16]{1,0:T(4,128)} %bitcast.11, s32[2,16,128]{2,1,0:T(8,128)} %bitcast.10, ...), custom_call_target="tpu_custom_call" | custom-call | tf_op jit(solution)/shard_map/state/pallas_call | solution.py:340
  3.8 0.0 copy-start
  3.8 3.1 %collective-permute-start.1 = (f32[2,128,128]{2,1,0:T(8,128)S(1)}, f32[2,128,128]{2,1,0:T(8,128)S(1)}, u32[]{:S(2)}, u32[]{:S(2)}) collective-permute-start(f32[2,128,128]{2,1,0:T(8,128)S(1)} %get-tuple-element.29), channel_id=1, source_target_pairs={{0,16},{8,24},{16,0},{24,8},{1,17},{9,25},{17,1},{25,9},{2,18},{10... | collective-permute-start | bytes 393224 | tf_op jit(solution)/shard_map/ppermute | solution.py:309
  6.9 3.5 %collective-permute-done.1 = f32[2,128,128]{2,1,0:T(8,128)S(1)} collective-permute-done((f32[2,128,128]{2,1,0:T(8,128)S(1)}, f32[2,128,128]{2,1,0:T(8,128)S(1)}, u32[]{:S(2)}, u32[]{:S(2)}) %collective-permute-start.1) | collective-permute-done | bytes 131104 | tf_op jit(solution)/shard_map/ppermute | solution.py:309
  10.4 0.5 %collective-permute-start = (f32[2,128,128]{2,1,0:T(8,128)S(1)}, f32[2,128,128]{2,1,0:T(8,128)S(1)}, u32[]{:S(2)}, u32[]{:S(2)}) collective-permute-start(f32[2,128,128]{2,1,0:T(8,128)S(1)} %get-tuple-element.29), channel_id=1, source_target_pairs={{0,8},{8,0},{16,24},{24,16},{1,9},{9,1},{17,25},{25,17},{2,10},{10... | collective-permute-start | bytes 393224 | tf_op jit(solution)/shard_map/ppermute | solution.py:309
  10.9 0.6 %scale.1.scaled_ref = f32[2,128,2048]{2,1,0:T(8,128)S(1)} custom-call(f32[2,2048,128]{2,1,0:T(8,128)S(1)} %copy-done.1, f32[1,128]{1,0:T(1,128)S(1)} %bitcast.7), custom_call_target="tpu_custom_call" | custom-call | tf_op jit(solution)/shard_map/scale/pallas_call | solution.py:391
  11.5 3.9 %local.1 = (bf16[2,256,2048]{2,1,0:T(8,128)(2,1)S(1)}, bf16[2,256,2048]{2,1,0:T(8,128)(2,1)S(1)}, f32[2,128,2048]{2,1,0:T(8,128)S(1)}) custom-call(f32[3,2,16,128]{3,2,1,0:T(8,128)S(1)} %get-tuple-element.18.weight_ref, f32[2,2048,128]{2,1,0:T(8,128)S(1)} %copy-done, bf16[2,2048,256]{2,1,0:T(8,128)(2,1)S(1)} %get-tuple-element.21.key_ref, ...), custom_call_target="tpu_custom_call" | custom-call | tf_op jit(solution)/shard_map/local/pallas_call | solution.py:378
  15.5 1.1 %combine.1 = (f32[2,128,2048]{2,1,0:T(8,128)S(1)}, f32[2,2,16,128]{3,2,1,0:T(8,128)S(1)}) custom-call(f32[2,128,2048]{2,1,0:T(8,128)S(1)} %get-tuple-element.24.local_ref, bf16[2,256,2048]{2,1,0:T(8,128)(2,1)S(1)} %get-tuple-element.25.high_ref, bf16[2,256,2048]{2,1,0:T(8,128)(2,1)S(1)} %get-tuple-element.26.low_ref, f32[2,128,2048]{2,1,0:T(8,128)S(1)} %scale.1.scaled_ref, ...), custom_call_target="tpu_custom_call" | custom-call | tf_op jit(solution)/shard_map/combine/pallas_call | solution.py:399
  16.6 1.8 %collective-permute-start.3 = (f32[2,2,16,128]{3,2,1,0:T(8,128)S(1)}, f32[2,2,16,128]{3,2,1,0:T(8,128)S(1)}, u32[]{:S(2)}, u32[]{:S(2)}) collective-permute-start(f32[2,2,16,128]{3,2,1,0:T(8,128)S(1)} %get-tuple-element.30), channel_id=1, source_target_pairs={{0,1},{1,0},{2,3},{3,2},{4,5},{5,4},{6,7},{7,6},{8,9},{9,8},{10,11... | collective-permute-start | bytes 98312 | tf_op jit(solution)/shard_map/ppermute | solution.py:314
  18.4 1.5 %collective-permute-start.4 = (f32[2,2,16,128]{3,2,1,0:T(8,128)S(1)}, f32[2,2,16,128]{3,2,1,0:T(8,128)S(1)}, u32[]{:S(2)}, u32[]{:S(2)}) collective-permute-start(f32[2,2,16,128]{3,2,1,0:T(8,128)S(1)} %get-tuple-element.30), channel_id=1, source_target_pairs={{0,3},{1,2},{2,1},{3,0},{4,7},{5,6},{6,5},{7,4},{8,11},{9,10},{10,... | collective-permute-start | bytes 98312 | tf_op jit(solution)/shard_map/ppermute | solution.py:314
  19.9 0.2 collective-permute-start.5
  20.2 0.4 %collective-permute-done.3 = f32[2,2,16,128]{3,2,1,0:T(8,128)S(1)} collective-permute-done((f32[2,2,16,128]{3,2,1,0:T(8,128)S(1)}, f32[2,2,16,128]{3,2,1,0:T(8,128)S(1)}, u32[]{:S(2)}, u32[]{:S(2)}) %collective-permute-start.3) | collective-permute-done | bytes 32800 | tf_op jit(solution)/shard_map/ppermute | solution.py:314
  20.6 2.9 %collective-permute-done.4 = f32[2,2,16,128]{3,2,1,0:T(8,128)S(1)} collective-permute-done((f32[2,2,16,128]{3,2,1,0:T(8,128)S(1)}, f32[2,2,16,128]{3,2,1,0:T(8,128)S(1)}, u32[]{:S(2)}, u32[]{:S(2)}) %collective-permute-start.4) | collective-permute-done | bytes 32800 | tf_op jit(solution)/shard_map/ppermute | solution.py:314
  23.5 0.3 collective-permute-done.5
  23.9 2.6 %collective-permute-start.6 = (f32[2,2,16,128]{3,2,1,0:T(8,128)S(1)}, f32[2,2,16,128]{3,2,1,0:T(8,128)S(1)}, u32[]{:S(2)}, u32[]{:S(2)}) collective-permute-start(f32[2,2,16,128]{3,2,1,0:T(8,128)S(1)} %add_add_fusion), channel_id=1, source_target_pairs={{0,4},{1,5},{2,6},{3,7},{4,0},{5,1},{6,2},{7,3},{8,12},{9,13},{10,... | collective-permute-start | bytes 98312 | tf_op jit(solution)/shard_map/ppermute | solution.py:314
  26.5 2.2 %collective-permute-done.6 = f32[2,2,16,128]{3,2,1,0:T(8,128)S(1)} collective-permute-done((f32[2,2,16,128]{3,2,1,0:T(8,128)S(1)}, f32[2,2,16,128]{3,2,1,0:T(8,128)S(1)}, u32[]{:S(2)}, u32[]{:S(2)}) %collective-permute-start.6) | collective-permute-done | bytes 32800 | tf_op jit(solution)/shard_map/ppermute | solution.py:314
  28.7 0.9 %top_gradient.1 = (f32[2,128,128]{2,1,0:T(8,128)S(1)}, bf16[2,256,2048]{2,1,0:T(8,128)(2,1)S(1)}) custom-call(f32[2,2,16,128]{3,2,1,0:T(8,128)S(1)} %add.19.sums_ref, f32[2,128,2048]{2,1,0:T(8,128)S(1)} %get-tuple-element.31.combined_ref, f32[2,128,2048]{2,1,0:T(8,128)S(1)} %scale.1.scaled_ref, bf16[2,256,2048]{2,1,0:T(8,128)(2,1)S(1)} %get-tuple-element.25.high_ref, ...), custom_call_target="tpu_custom_call" | custom-call | tf_op jit(solution)/shard_map/top_gradient/pallas_call | solution.py:416
  29.7 1.6 %collective-permute-start.7 = (f32[2,128,128]{2,1,0:T(8,128)S(1)}, f32[2,128,128]{2,1,0:T(8,128)S(1)}, u32[]{:S(2)}, u32[]{:S(2)}) collective-permute-start(f32[2,128,128]{2,1,0:T(8,128)S(1)} %get-tuple-element.32), channel_id=1, source_target_pairs={{0,16},{8,24},{16,0},{24,8},{1,17},{9,25},{17,1},{25,9},{2,18},{10... | collective-permute-start | bytes 393224 | tf_op jit(solution)/shard_map/ppermute | solution.py:309
  31.3 0.8 %rest_gradient.1 = f32[2,128,128]{2,1,0:T(8,128)S(1)} custom-call(bf16[2,256,2048]{2,1,0:T(8,128)(2,1)S(1)} %get-tuple-element.33.parts_ref, bf16[2,256,2048]{2,1,0:T(8,128)(2,1)S(1)} %get-tuple-element.25.high_ref, bf16[2,256,2048]{2,1,0:T(8,128)(2,1)S(1)} %get-tuple-element.26.low_ref), custom_call_target="tpu_custom_call" | custom-call | tf_op jit(solution)/shard_map/rest_gradient/pallas_call | solution.py:423
  32.1 0.1 collective-permute-start.9
  32.1 2.6 %collective-permute-done.7.refs_0_ = f32[2,128,128]{2,1,0:T(8,128)S(1)} collective-permute-done((f32[2,128,128]{2,1,0:T(8,128)S(1)}, f32[2,128,128]{2,1,0:T(8,128)S(1)}, u32[]{:S(2)}, u32[]{:S(2)}) %collective-permute-start.7) | collective-permute-done | bytes 131104 | tf_op jit(solution)/shard_map/ppermute | solution.py:309
  34.7 0.0 collective-permute-start.8
  34.7 1.6 %attended.1 = f32[2,2048,128]{2,1,0:T(8,128)} custom-call(f32[2,2,16,128]{3,2,1,0:T(8,128)S(1)} %add.19.sums_ref, f32[2,128,2048]{2,1,0:T(8,128)S(1)} %get-tuple-element.31.combined_ref, f32[1,128]{1,0:T(1,128)S(1)} %bitcast.8), custom_call_target="tpu_custom_call" | custom-call | tf_op jit(solution)/shard_map/attended/pallas_call | solution.py:431
  36.3 0.7 %finish.1 = f32[2,128,128]{2,1,0:T(8,128)} custom-call(f32[2,128,128]{2,1,0:T(8,128)S(1)} %collective-permute-done.7.refs_0_, f32[2,128,128]{2,1,0:T(8,128)S(1)} %collective-permute-done.8.refs_1_, f32[2,128,128]{2,1,0:T(8,128)S(1)} %collective-permute-done.9.refs_2_), custom_call_target="tpu_custom_call" | custom-call | tf_op jit(solution)/shard_map/finish/pallas_call | solution.py:449
  (13 shorter events, 0.1 us)
Async XLA Ops:
  0.6 10.3 %copy-start.1 = (f32[2,2048,128]{2,1,0:T(8,128)S(1)}, f32[2,2048,128]{2,1,0:T(8,128)}, u32[]{:S(2)}) copy-start(f32[2,2048,128]{2,1,0:T(8,128)} %cotangent_ref) | copy-start | bytes 6291460
  0.6 10.3 %copy-start.2 = (f32[128]{0:T(128)S(1)}, f32[128]{0:T(128)}, u32[]{:S(2)}) copy-start(f32[128]{0:T(128)} %param.15) | copy-start | bytes 1540
  3.8 7.7 %copy-start = (f32[2,2048,128]{2,1,0:T(8,128)S(1)}, f32[2,2048,128]{2,1,0:T(8,128)}, u32[]{:S(2)}) copy-start(f32[2,2048,128]{2,1,0:T(8,128)} %query_ref) | copy-start | bytes 6291460
  3.8 6.6 %collective-permute-start.1 = (f32[2,128,128]{2,1,0:T(8,128)S(1)}, f32[2,128,128]{2,1,0:T(8,128)S(1)}, u32[]{:S(2)}, u32[]{:S(2)}) collective-permute-start(f32[2,128,128]{2,1,0:T(8,128)S(1)} %get-tuple-element.29), channel_id=1, source_target_pairs={{0,16},{8,24},{16,0},{24,8},{1,17},{9,25},{17,1},{25,9},{2,18},{10... | collective-permute-start | bytes 393224 | tf_op jit(solution)/shard_map/ppermute | solution.py:309
  10.4 5.0 %collective-permute-start.2 = (f32[2,128,128]{2,1,0:T(8,128)S(1)}, f32[2,128,128]{2,1,0:T(8,128)S(1)}, u32[]{:S(2)}, u32[]{:S(2)}) collective-permute-start(f32[2,128,128]{2,1,0:T(8,128)S(1)} %collective-permute-done.1), channel_id=1, source_target_pairs={{0,8},{8,0},{16,24},{24,16},{1,9},{9,1},{17,25},{25,17},{2,10},{10... | collective-permute-start | bytes 393224 | tf_op jit(solution)/shard_map/ppermute | solution.py:309
  10.4 5.1 %collective-permute-start = (f32[2,128,128]{2,1,0:T(8,128)S(1)}, f32[2,128,128]{2,1,0:T(8,128)S(1)}, u32[]{:S(2)}, u32[]{:S(2)}) collective-permute-start(f32[2,128,128]{2,1,0:T(8,128)S(1)} %get-tuple-element.29), channel_id=1, source_target_pairs={{0,8},{8,0},{16,24},{24,16},{1,9},{9,1},{17,25},{25,17},{2,10},{10... | collective-permute-start | bytes 393224 | tf_op jit(solution)/shard_map/ppermute | solution.py:309
  16.6 4.0 %collective-permute-start.3 = (f32[2,2,16,128]{3,2,1,0:T(8,128)S(1)}, f32[2,2,16,128]{3,2,1,0:T(8,128)S(1)}, u32[]{:S(2)}, u32[]{:S(2)}) collective-permute-start(f32[2,2,16,128]{3,2,1,0:T(8,128)S(1)} %get-tuple-element.30), channel_id=1, source_target_pairs={{0,1},{1,0},{2,3},{3,2},{4,5},{5,4},{6,7},{7,6},{8,9},{9,8},{10,11... | collective-permute-start | bytes 98312 | tf_op jit(solution)/shard_map/ppermute | solution.py:314
  18.4 5.1 %collective-permute-start.4 = (f32[2,2,16,128]{3,2,1,0:T(8,128)S(1)}, f32[2,2,16,128]{3,2,1,0:T(8,128)S(1)}, u32[]{:S(2)}, u32[]{:S(2)}) collective-permute-start(f32[2,2,16,128]{3,2,1,0:T(8,128)S(1)} %get-tuple-element.30), channel_id=1, source_target_pairs={{0,3},{1,2},{2,1},{3,0},{4,7},{5,6},{6,5},{7,4},{8,11},{9,10},{10,... | collective-permute-start | bytes 98312 | tf_op jit(solution)/shard_map/ppermute | solution.py:314
  19.9 3.9 %collective-permute-start.5 = (f32[2,2,16,128]{3,2,1,0:T(8,128)S(1)}, f32[2,2,16,128]{3,2,1,0:T(8,128)S(1)}, u32[]{:S(2)}, u32[]{:S(2)}) collective-permute-start(f32[2,2,16,128]{3,2,1,0:T(8,128)S(1)} %get-tuple-element.30), channel_id=1, source_target_pairs={{0,2},{1,3},{2,0},{3,1},{4,6},{5,7},{6,4},{7,5},{8,10},{9,11},{10,... | collective-permute-start | bytes 98312 | tf_op jit(solution)/shard_map/ppermute | solution.py:314
  23.9 4.9 %collective-permute-start.6 = (f32[2,2,16,128]{3,2,1,0:T(8,128)S(1)}, f32[2,2,16,128]{3,2,1,0:T(8,128)S(1)}, u32[]{:S(2)}, u32[]{:S(2)}) collective-permute-start(f32[2,2,16,128]{3,2,1,0:T(8,128)S(1)} %add_add_fusion), channel_id=1, source_target_pairs={{0,4},{1,5},{2,6},{3,7},{4,0},{5,1},{6,2},{7,3},{8,12},{9,13},{10,... | collective-permute-start | bytes 98312 | tf_op jit(solution)/shard_map/ppermute | solution.py:314
  29.7 5.0 %collective-permute-start.7 = (f32[2,128,128]{2,1,0:T(8,128)S(1)}, f32[2,128,128]{2,1,0:T(8,128)S(1)}, u32[]{:S(2)}, u32[]{:S(2)}) collective-permute-start(f32[2,128,128]{2,1,0:T(8,128)S(1)} %get-tuple-element.32), channel_id=1, source_target_pairs={{0,16},{8,24},{16,0},{24,8},{1,17},{9,25},{17,1},{25,9},{2,18},{10... | collective-permute-start | bytes 393224 | tf_op jit(solution)/shard_map/ppermute | solution.py:309
  32.1 4.2 %collective-permute-start.9 = (f32[2,128,128]{2,1,0:T(8,128)S(1)}, f32[2,128,128]{2,1,0:T(8,128)S(1)}, u32[]{:S(2)}, u32[]{:S(2)}) collective-permute-start(f32[2,128,128]{2,1,0:T(8,128)S(1)} %rest_gradient.1), channel_id=1, source_target_pairs={{0,8},{8,0},{16,24},{24,16},{1,9},{9,1},{17,25},{25,17},{2,10},{10... | collective-permute-start | bytes 393224 | tf_op jit(solution)/shard_map/ppermute | solution.py:309
  34.7 1.6 %collective-permute-start.8 = (f32[2,128,128]{2,1,0:T(8,128)S(1)}, f32[2,128,128]{2,1,0:T(8,128)S(1)}, u32[]{:S(2)}, u32[]{:S(2)}) collective-permute-start(f32[2,128,128]{2,1,0:T(8,128)S(1)} %collective-permute-done.7.refs_0_), channel_id=1, source_target_pairs={{0,8},{8,0},{16,24},{24,16},{1,9},{9,1},{17,25},{25,17},{2,10},{10... | collective-permute-start | bytes 393224 | tf_op jit(solution)/shard_map/ppermute | solution.py:309

commit v3 on v2

--- a/solution.py
+++ b/solution.py
@@ -30,18 +30,17 @@
     return high, (array - high.astype(F32)).astype(BF16)
 
 
-def chunk_states(groups, tokens, spans, key_at, value_at, outs, ready=None):
+def chunk_states(groups, tokens, span_at, key_at, value_at, outs, ready):
     key_out, value_out, prefix_out, state_out = outs
     spots = [(group, chunk) for group in range(groups) for chunk in range(tokens // CHUNK)]
 
     def prepare(group, chunk):
-        if ready is not None:
-            ready(group, chunk)
+        ready(group, chunk)
         rows = pl.ds(chunk * CHUNK, CHUNK)
         live = key_at(group, rows)
         if (chunk + 1) * CHUNK > tokens // 2:
             position = lax.broadcasted_iota(jnp.int32, (CHUNK, DH), 0)
-            live = jnp.where(position < spans[group] - chunk * CHUNK, live, 0.0)
+            live = jnp.where(position < span_at(group) - chunk * CHUNK, live, 0.0)
         key_out[group, rows, :] = jnp.concatenate(halves(live), axis=1)
         value_out[group, :, rows] = jnp.concatenate(halves(value_at(group, rows).T), axis=0)
 
@@ -97,13 +96,14 @@
             ]
             for copy in loads[group, load]:
                 copy.start()
-    small[0].wait()
 
     def ready(group, chunk):
         if chunk * CHUNK % LOAD == 0:
             for copy in loads[group, chunk * CHUNK // LOAD]:
                 copy.wait()
-        if group == 0 and (chunk + 1) * CHUNK == tokens:
+        if group == 0 and chunk == tokens // 2 // CHUNK:
+            small[0].wait()
+        if group == groups // 2 and chunk == 0:
             for copy in small[1:]:
                 copy.wait()
             level_weights(table_ref, selector_ref, weight_out)
@@ -111,7 +111,7 @@
     chunk_states(
         groups,
         tokens,
-        [span_ref[group // heads] for group in range(groups)],
+        lambda group: span_ref[group // heads],
         lambda group, rows: key_ref[group, rows, :],
         lambda group, rows: value_ref[group, rows, :],
         outs,

time: 37.1 us -> 37 us (level)
  no operation moved by 1% of the time
where the time goes in v3:
time: 37 us; the launch traced here: 36.8 us
  Pallas kernels  12.6 us (34%)
  waiting for transfers between devices  12 us (32%)
  starting transfers between devices  11.4 us (31%)
  between operations  0.78 us (2%)
    ppermute x4, starting transfers between devices, exchange(): lax.ppermute(shard, axis, [(i, i ^ mask) for i in range(size)])  6.21 us
    ppermute x6, waiting for transfers between devices, partner(): lax.ppermute(shard, axis, [(i, i ^ 1 << stride) for i in range(lax.axis_s...  6.06 us
    ppermute x4, waiting for transfers between devices, exchange(): lax.ppermute(shard, axis, [(i, i ^ mask) for i in range(size)])  5.91 us
    ppermute x6, starting transfers between devices, partner(): lax.ppermute(shard, axis, [(i, i ^ 1 << stride) for i in range(lax.axis_s...  5.23 us
    pallas_call x1, Pallas kernels, body(): call(local_kernel, out_shape=(resident((groups, stacked, tokens), BF16),...  3.88 us
    pallas_call x1, Pallas kernels, body(): call(functools.partial(state_kernel, heads), out_shape=(resident((groups,...  3 us
    pallas_call x1, Pallas kernels, body(): call(functools.partial(attended_kernel, heads, full_width), out_shape=jax...  1.56 us
    pallas_call x1, Pallas kernels, body(): call(functools.partial(combine_kernel, heads), out_shape=(resident((group...  1.12 us
  transfers between devices with their start and end apart: 10, of which 6 were waited for; matrix products, arithmetic and copies ran while one was open for 0% of the time, Pallas kernels for 19%

profile of v3, /device:TPU:0, one launch (start us, length us, event | category | flops | bytes accessed | tf_op | source)
XLA Modules:
  0.0 36.8 jit_solution(2253112050080786735)
XLA Ops:
  0.7 3.0 %state.1 = (bf16[2,2048,256]{2,1,0:T(8,128)(2,1)S(1)}, bf16[2,256,2048]{2,1,0:T(8,128)(2,1)S(1)}, f32[2,8,128,128]{3,2,1,0:T(8,128)S(1)}, f32[2,128,128]{2,1,0:T(8,128)S(1)}, f32[3,2,16,128]{3,2,1,0:T(8,128)S(1)}) custom-call(s32[2]{0:T(128)} %bitcast.12, f32[3,16]{1,0:T(4,128)} %bitcast.11, s32[2,16,128]{2,1,0:T(8,128)} %bitcast.10, ...), custom_call_target="tpu_custom_call" | custom-call | tf_op jit(solution)/shard_map/state/pallas_call | solution.py:340
  3.7 0.0 copy-start
  3.7 3.1 %collective-permute-start.1 = (f32[2,128,128]{2,1,0:T(8,128)S(1)}, f32[2,128,128]{2,1,0:T(8,128)S(1)}, u32[]{:S(2)}, u32[]{:S(2)}) collective-permute-start(f32[2,128,128]{2,1,0:T(8,128)S(1)} %get-tuple-element.29), channel_id=1, source_target_pairs={{0,16},{8,24},{16,0},{24,8},{1,17},{9,25},{17,1},{25,9},{2,18},{10... | collective-permute-start | bytes 393224 | tf_op jit(solution)/shard_map/ppermute | solution.py:309
  6.7 3.5 %collective-permute-done.1 = f32[2,128,128]{2,1,0:T(8,128)S(1)} collective-permute-done((f32[2,128,128]{2,1,0:T(8,128)S(1)}, f32[2,128,128]{2,1,0:T(8,128)S(1)}, u32[]{:S(2)}, u32[]{:S(2)}) %collective-permute-start.1) | collective-permute-done | bytes 131104 | tf_op jit(solution)/shard_map/ppermute | solution.py:309
  10.2 0.0 collective-permute-start.2
  10.2 0.5 %collective-permute-start = (f32[2,128,128]{2,1,0:T(8,128)S(1)}, f32[2,128,128]{2,1,0:T(8,128)S(1)}, u32[]{:S(2)}, u32[]{:S(2)}) collective-permute-start(f32[2,128,128]{2,1,0:T(8,128)S(1)} %get-tuple-element.29), channel_id=1, source_target_pairs={{0,8},{8,0},{16,24},{24,16},{1,9},{9,1},{17,25},{25,17},{2,10},{10... | collective-permute-start | bytes 393224 | tf_op jit(solution)/shard_map/ppermute | solution.py:309
  10.7 0.6 %scale.1.scaled_ref = f32[2,128,2048]{2,1,0:T(8,128)S(1)} custom-call(f32[2,2048,128]{2,1,0:T(8,128)S(1)} %copy-done.1, f32[1,128]{1,0:T(1,128)S(1)} %bitcast.7), custom_call_target="tpu_custom_call" | custom-call | tf_op jit(solution)/shard_map/scale/pallas_call | solution.py:391
  11.4 3.9 %local.1 = (bf16[2,256,2048]{2,1,0:T(8,128)(2,1)S(1)}, bf16[2,256,2048]{2,1,0:T(8,128)(2,1)S(1)}, f32[2,128,2048]{2,1,0:T(8,128)S(1)}) custom-call(f32[3,2,16,128]{3,2,1,0:T(8,128)S(1)} %get-tuple-element.18.weight_ref, f32[2,2048,128]{2,1,0:T(8,128)S(1)} %copy-done, bf16[2,2048,256]{2,1,0:T(8,128)(2,1)S(1)} %get-tuple-element.21.key_ref, ...), custom_call_target="tpu_custom_call" | custom-call | tf_op jit(solution)/shard_map/local/pallas_call | solution.py:378
  15.3 1.1 %combine.1 = (f32[2,128,2048]{2,1,0:T(8,128)S(1)}, f32[2,2,16,128]{3,2,1,0:T(8,128)S(1)}) custom-call(f32[2,128,2048]{2,1,0:T(8,128)S(1)} %get-tuple-element.24.local_ref, bf16[2,256,2048]{2,1,0:T(8,128)(2,1)S(1)} %get-tuple-element.25.high_ref, bf16[2,256,2048]{2,1,0:T(8,128)(2,1)S(1)} %get-tuple-element.26.low_ref, f32[2,128,2048]{2,1,0:T(8,128)S(1)} %scale.1.scaled_ref, ...), custom_call_target="tpu_custom_call" | custom-call | tf_op jit(solution)/shard_map/combine/pallas_call | solution.py:399
  16.4 1.8 %collective-permute-start.3 = (f32[2,2,16,128]{3,2,1,0:T(8,128)S(1)}, f32[2,2,16,128]{3,2,1,0:T(8,128)S(1)}, u32[]{:S(2)}, u32[]{:S(2)}) collective-permute-start(f32[2,2,16,128]{3,2,1,0:T(8,128)S(1)} %get-tuple-element.30), channel_id=1, source_target_pairs={{0,1},{1,0},{2,3},{3,2},{4,5},{5,4},{6,7},{7,6},{8,9},{9,8},{10,11... | collective-permute-start | bytes 98312 | tf_op jit(solution)/shard_map/ppermute | solution.py:314
  18.2 1.6 %collective-permute-start.4 = (f32[2,2,16,128]{3,2,1,0:T(8,128)S(1)}, f32[2,2,16,128]{3,2,1,0:T(8,128)S(1)}, u32[]{:S(2)}, u32[]{:S(2)}) collective-permute-start(f32[2,2,16,128]{3,2,1,0:T(8,128)S(1)} %get-tuple-element.30), channel_id=1, source_target_pairs={{0,3},{1,2},{2,1},{3,0},{4,7},{5,6},{6,5},{7,4},{8,11},{9,10},{10,... | collective-permute-start | bytes 98312 | tf_op jit(solution)/shard_map/ppermute | solution.py:314
  19.8 0.2 collective-permute-start.5
  20.0 0.4 %collective-permute-done.3 = f32[2,2,16,128]{3,2,1,0:T(8,128)S(1)} collective-permute-done((f32[2,2,16,128]{3,2,1,0:T(8,128)S(1)}, f32[2,2,16,128]{3,2,1,0:T(8,128)S(1)}, u32[]{:S(2)}, u32[]{:S(2)}) %collective-permute-start.3) | collective-permute-done | bytes 32800 | tf_op jit(solution)/shard_map/ppermute | solution.py:314
  20.4 2.9 %collective-permute-done.4 = f32[2,2,16,128]{3,2,1,0:T(8,128)S(1)} collective-permute-done((f32[2,2,16,128]{3,2,1,0:T(8,128)S(1)}, f32[2,2,16,128]{3,2,1,0:T(8,128)S(1)}, u32[]{:S(2)}, u32[]{:S(2)}) %collective-permute-start.4) | collective-permute-done | bytes 32800 | tf_op jit(solution)/shard_map/ppermute | solution.py:314
  23.3 0.4 collective-permute-done.5
  23.7 2.7 %collective-permute-start.6 = (f32[2,2,16,128]{3,2,1,0:T(8,128)S(1)}, f32[2,2,16,128]{3,2,1,0:T(8,128)S(1)}, u32[]{:S(2)}, u32[]{:S(2)}) collective-permute-start(f32[2,2,16,128]{3,2,1,0:T(8,128)S(1)} %add_add_fusion), channel_id=1, source_target_pairs={{0,4},{1,5},{2,6},{3,7},{4,0},{5,1},{6,2},{7,3},{8,12},{9,13},{10,... | collective-permute-start | bytes 98312 | tf_op jit(solution)/shard_map/ppermute | solution.py:314
  26.3 2.2 %collective-permute-done.6 = f32[2,2,16,128]{3,2,1,0:T(8,128)S(1)} collective-permute-done((f32[2,2,16,128]{3,2,1,0:T(8,128)S(1)}, f32[2,2,16,128]{3,2,1,0:T(8,128)S(1)}, u32[]{:S(2)}, u32[]{:S(2)}) %collective-permute-start.6) | collective-permute-done | bytes 32800 | tf_op jit(solution)/shard_map/ppermute | solution.py:314
  28.6 0.9 %top_gradient.1 = (f32[2,128,128]{2,1,0:T(8,128)S(1)}, bf16[2,256,2048]{2,1,0:T(8,128)(2,1)S(1)}) custom-call(f32[2,2,16,128]{3,2,1,0:T(8,128)S(1)} %add.19.sums_ref, f32[2,128,2048]{2,1,0:T(8,128)S(1)} %get-tuple-element.31.combined_ref, f32[2,128,2048]{2,1,0:T(8,128)S(1)} %scale.1.scaled_ref, bf16[2,256,2048]{2,1,0:T(8,128)(2,1)S(1)} %get-tuple-element.25.high_ref, ...), custom_call_target="tpu_custom_call" | custom-call | tf_op jit(solution)/shard_map/top_gradient/pallas_call | solution.py:416
  29.5 1.6 %collective-permute-start.7 = (f32[2,128,128]{2,1,0:T(8,128)S(1)}, f32[2,128,128]{2,1,0:T(8,128)S(1)}, u32[]{:S(2)}, u32[]{:S(2)}) collective-permute-start(f32[2,128,128]{2,1,0:T(8,128)S(1)} %get-tuple-element.32), channel_id=1, source_target_pairs={{0,16},{8,24},{16,0},{24,8},{1,17},{9,25},{17,1},{25,9},{2,18},{10... | collective-permute-start | bytes 393224 | tf_op jit(solution)/shard_map/ppermute | solution.py:309
  31.1 0.8 %rest_gradient.1 = f32[2,128,128]{2,1,0:T(8,128)S(1)} custom-call(bf16[2,256,2048]{2,1,0:T(8,128)(2,1)S(1)} %get-tuple-element.33.parts_ref, bf16[2,256,2048]{2,1,0:T(8,128)(2,1)S(1)} %get-tuple-element.25.high_ref, bf16[2,256,2048]{2,1,0:T(8,128)(2,1)S(1)} %get-tuple-element.26.low_ref), custom_call_target="tpu_custom_call" | custom-call | tf_op jit(solution)/shard_map/rest_gradient/pallas_call | solution.py:423
  31.9 0.1 collective-permute-start.9
  32.0 2.6 %collective-permute-done.7.refs_0_ = f32[2,128,128]{2,1,0:T(8,128)S(1)} collective-permute-done((f32[2,128,128]{2,1,0:T(8,128)S(1)}, f32[2,128,128]{2,1,0:T(8,128)S(1)}, u32[]{:S(2)}, u32[]{:S(2)}) %collective-permute-start.7) | collective-permute-done | bytes 131104 | tf_op jit(solution)/shard_map/ppermute | solution.py:309
  34.5 1.6 %attended.1 = f32[2,2048,128]{2,1,0:T(8,128)} custom-call(f32[2,2,16,128]{3,2,1,0:T(8,128)S(1)} %add.19.sums_ref, f32[2,128,2048]{2,1,0:T(8,128)S(1)} %get-tuple-element.31.combined_ref, f32[1,128]{1,0:T(1,128)S(1)} %bitcast.8), custom_call_target="tpu_custom_call" | custom-call | tf_op jit(solution)/shard_map/attended/pallas_call | solution.py:431
  36.1 0.7 %finish.1 = f32[2,128,128]{2,1,0:T(8,128)} custom-call(f32[2,128,128]{2,1,0:T(8,128)S(1)} %collective-permute-done.7.refs_0_, f32[2,128,128]{2,1,0:T(8,128)S(1)} %collective-permute-done.8.refs_1_, f32[2,128,128]{2,1,0:T(8,128)S(1)} %collective-permute-done.9.refs_2_), custom_call_target="tpu_custom_call" | custom-call | tf_op jit(solution)/shard_map/finish/pallas_call | solution.py:449
  (13 shorter events, 0.1 us)
Async XLA Ops:
  0.6 10.1 %copy-start.1 = (f32[2,2048,128]{2,1,0:T(8,128)S(1)}, f32[2,2048,128]{2,1,0:T(8,128)}, u32[]{:S(2)}) copy-start(f32[2,2048,128]{2,1,0:T(8,128)} %cotangent_ref) | copy-start | bytes 6291460
  0.6 10.1 %copy-start.2 = (f32[128]{0:T(128)S(1)}, f32[128]{0:T(128)}, u32[]{:S(2)}) copy-start(f32[128]{0:T(128)} %param.15) | copy-start | bytes 1540
  3.7 7.7 %copy-start = (f32[2,2048,128]{2,1,0:T(8,128)S(1)}, f32[2,2048,128]{2,1,0:T(8,128)}, u32[]{:S(2)}) copy-start(f32[2,2048,128]{2,1,0:T(8,128)} %query_ref) | copy-start | bytes 6291460
  3.7 6.6 %collective-permute-start.1 = (f32[2,128,128]{2,1,0:T(8,128)S(1)}, f32[2,128,128]{2,1,0:T(8,128)S(1)}, u32[]{:S(2)}, u32[]{:S(2)}) collective-permute-start(f32[2,128,128]{2,1,0:T(8,128)S(1)} %get-tuple-element.29), channel_id=1, source_target_pairs={{0,16},{8,24},{16,0},{24,8},{1,17},{9,25},{17,1},{25,9},{2,18},{10... | collective-permute-start | bytes 393224 | tf_op jit(solution)/shard_map/ppermute | solution.py:309
  10.2 5.0 %collective-permute-start.2 = (f32[2,128,128]{2,1,0:T(8,128)S(1)}, f32[2,128,128]{2,1,0:T(8,128)S(1)}, u32[]{:S(2)}, u32[]{:S(2)}) collective-permute-start(f32[2,128,128]{2,1,0:T(8,128)S(1)} %collective-permute-done.1), channel_id=1, source_target_pairs={{0,8},{8,0},{16,24},{24,16},{1,9},{9,1},{17,25},{25,17},{2,10},{10... | collective-permute-start | bytes 393224 | tf_op jit(solution)/shard_map/ppermute | solution.py:309
  10.2 5.1 %collective-permute-start = (f32[2,128,128]{2,1,0:T(8,128)S(1)}, f32[2,128,128]{2,1,0:T(8,128)S(1)}, u32[]{:S(2)}, u32[]{:S(2)}) collective-permute-start(f32[2,128,128]{2,1,0:T(8,128)S(1)} %get-tuple-element.29), channel_id=1, source_target_pairs={{0,8},{8,0},{16,24},{24,16},{1,9},{9,1},{17,25},{25,17},{2,10},{10... | collective-permute-start | bytes 393224 | tf_op jit(solution)/shard_map/ppermute | solution.py:309
  16.4 4.0 %collective-permute-start.3 = (f32[2,2,16,128]{3,2,1,0:T(8,128)S(1)}, f32[2,2,16,128]{3,2,1,0:T(8,128)S(1)}, u32[]{:S(2)}, u32[]{:S(2)}) collective-permute-start(f32[2,2,16,128]{3,2,1,0:T(8,128)S(1)} %get-tuple-element.30), channel_id=1, source_target_pairs={{0,1},{1,0},{2,3},{3,2},{4,5},{5,4},{6,7},{7,6},{8,9},{9,8},{10,11... | collective-permute-start | bytes 98312 | tf_op jit(solution)/shard_map/ppermute | solution.py:314
  18.2 5.1 %collective-permute-start.4 = (f32[2,2,16,128]{3,2,1,0:T(8,128)S(1)}, f32[2,2,16,128]{3,2,1,0:T(8,128)S(1)}, u32[]{:S(2)}, u32[]{:S(2)}) collective-permute-start(f32[2,2,16,128]{3,2,1,0:T(8,128)S(1)} %get-tuple-element.30), channel_id=1, source_target_pairs={{0,3},{1,2},{2,1},{3,0},{4,7},{5,6},{6,5},{7,4},{8,11},{9,10},{10,... | collective-permute-start | bytes 98312 | tf_op jit(solution)/shard_map/ppermute | solution.py:314
  19.8 3.9 %collective-permute-start.5 = (f32[2,2,16,128]{3,2,1,0:T(8,128)S(1)}, f32[2,2,16,128]{3,2,1,0:T(8,128)S(1)}, u32[]{:S(2)}, u32[]{:S(2)}) collective-permute-start(f32[2,2,16,128]{3,2,1,0:T(8,128)S(1)} %get-tuple-element.30), channel_id=1, source_target_pairs={{0,2},{1,3},{2,0},{3,1},{4,6},{5,7},{6,4},{7,5},{8,10},{9,11},{10,... | collective-permute-start | bytes 98312 | tf_op jit(solution)/shard_map/ppermute | solution.py:314
  23.7 4.9 %collective-permute-start.6 = (f32[2,2,16,128]{3,2,1,0:T(8,128)S(1)}, f32[2,2,16,128]{3,2,1,0:T(8,128)S(1)}, u32[]{:S(2)}, u32[]{:S(2)}) collective-permute-start(f32[2,2,16,128]{3,2,1,0:T(8,128)S(1)} %add_add_fusion), channel_id=1, source_target_pairs={{0,4},{1,5},{2,6},{3,7},{4,0},{5,1},{6,2},{7,3},{8,12},{9,13},{10,... | collective-permute-start | bytes 98312 | tf_op jit(solution)/shard_map/ppermute | solution.py:314
  29.5 5.0 %collective-permute-start.7 = (f32[2,128,128]{2,1,0:T(8,128)S(1)}, f32[2,128,128]{2,1,0:T(8,128)S(1)}, u32[]{:S(2)}, u32[]{:S(2)}) collective-permute-start(f32[2,128,128]{2,1,0:T(8,128)S(1)} %get-tuple-element.32), channel_id=1, source_target_pairs={{0,16},{8,24},{16,0},{24,8},{1,17},{9,25},{17,1},{25,9},{2,18},{10... | collective-permute-start | bytes 393224 | tf_op jit(solution)/shard_map/ppermute | solution.py:309
  31.9 4.2 %collective-permute-start.9 = (f32[2,128,128]{2,1,0:T(8,128)S(1)}, f32[2,128,128]{2,1,0:T(8,128)S(1)}, u32[]{:S(2)}, u32[]{:S(2)}) collective-permute-start(f32[2,128,128]{2,1,0:T(8,128)S(1)} %rest_gradient.1), channel_id=1, source_target_pairs={{0,8},{8,0},{16,24},{24,16},{1,9},{9,1},{17,25},{25,17},{2,10},{10... | collective-permute-start | bytes 393224 | tf_op jit(solution)/shard_map/ppermute | solution.py:309
  34.5 1.6 %collective-permute-start.8 = (f32[2,128,128]{2,1,0:T(8,128)S(1)}, f32[2,128,128]{2,1,0:T(8,128)S(1)}, u32[]{:S(2)}, u32[]{:S(2)}) collective-permute-start(f32[2,128,128]{2,1,0:T(8,128)S(1)} %collective-permute-done.7.refs_0_), channel_id=1, source_target_pairs={{0,8},{8,0},{16,24},{24,16},{1,9},{9,1},{17,25},{25,17},{2,10},{10... | collective-permute-start | bytes 393224 | tf_op jit(solution)/shard_map/ppermute | solution.py:309

commit v4 on v3

--- a/solution.py
+++ b/solution.py
@@ -10,7 +10,7 @@
 DH = 128
 LANES = 128
 CHUNK = 256
-LOAD = 1024
+LOAD = 2048
 EPSILON = 1e-06
 GRANT = 8 << 20
 F32, BF16 = jnp.float32, jnp.bfloat16
@@ -358,6 +358,7 @@
             pltpu.SemaphoreType.DMA((2, groups, tokens // LOAD)),
         ],
         name="state",
+        compiler_params=pltpu.CompilerParams(vmem_limit_bytes=GRANT),
     )(
         *map(
             leave,
@@ -386,6 +387,7 @@
         out_specs=(VMEM,) * 3,
         scratch_shapes=[pltpu.VMEM((2, DH, CHUNK), BF16)] * 2,
         name="local",
+        compiler_params=pltpu.CompilerParams(vmem_limit_bytes=GRANT),
     )(*map(keep, (weights, queries, key_parts, value_parts, prefixes)))
 
     scaled = call(
@@ -408,8 +410,8 @@
     )(*map(keep, (local_sum, weighted_high, weighted_low, scaled, *buckets)))
 
     head_bits = lax.axis_size("head").bit_length() - 1
-    rounds = [(1, 3, 2)[: (1 << min(2, head_bits)) - 1]]
-    rounds += [(1 << level,) for level in range(2, head_bits)]
+    rounds = [(1 << level,) for level in reversed(range(2, head_bits))]
+    rounds += [(1, 3, 2)[: (1 << min(2, head_bits)) - 1]]
     for masks in rounds:
         sums = exchange(sums, "head", masks)
 

time: 37 us -> 37.2 us (level)
  waiting for transfers between devices: 12 us -> 11.6 us
where the time goes in v4:
time: 37.2 us; the launch traced here: 37 us
  Pallas kernels  12.8 us (34%)
  starting transfers between devices  11.7 us (31%)
  waiting for transfers between devices  11.6 us (31%)
  between operations  0.78 us (2%)
    ppermute x4, starting transfers between devices, exchange(): lax.ppermute(shard, axis, [(i, i ^ mask) for i in range(size)])  6.46 us
    ppermute x6, waiting for transfers between devices, partner(): lax.ppermute(shard, axis, [(i, i ^ 1 << stride) for i in range(lax.axis_s...  6.06 us
    ppermute x4, waiting for transfers between devices, exchange(): lax.ppermute(shard, axis, [(i, i ^ mask) for i in range(size)])  5.59 us
    ppermute x6, starting transfers between devices, partner(): lax.ppermute(shard, axis, [(i, i ^ 1 << stride) for i in range(lax.axis_s...  5.23 us
    pallas_call x1, Pallas kernels, body(): call(local_kernel, out_shape=(resident((groups, stacked, tokens), BF16),...  3.89 us
    pallas_call x1, Pallas kernels, body(): call(functools.partial(state_kernel, heads), out_shape=(resident((groups,...  3.14 us
    pallas_call x1, Pallas kernels, body(): call(functools.partial(attended_kernel, heads, full_width), out_shape=jax...  1.68 us
    pallas_call x1, Pallas kernels, body(): call(functools.partial(combine_kernel, heads), out_shape=(resident((group...  1.12 us
  transfers between devices with their start and end apart: 10, of which 6 were waited for; matrix products, arithmetic and copies ran while one was open for 0% of the time, Pallas kernels for 19%

profile of v4, /device:TPU:0, one launch (start us, length us, event | category | flops | bytes accessed | tf_op | source)
XLA Modules:
  0.0 37.0 jit_solution(4650662304953636638)
XLA Ops:
  0.7 3.1 %state.1 = (bf16[2,2048,256]{2,1,0:T(8,128)(2,1)S(1)}, bf16[2,256,2048]{2,1,0:T(8,128)(2,1)S(1)}, f32[2,8,128,128]{3,2,1,0:T(8,128)S(1)}, f32[2,128,128]{2,1,0:T(8,128)S(1)}, f32[3,2,16,128]{3,2,1,0:T(8,128)S(1)}) custom-call(s32[2]{0:T(128)} %bitcast.12, f32[3,16]{1,0:T(4,128)} %bitcast.11, s32[2,16,128]{2,1,0:T(8,128)} %bitcast.10, ...), custom_call_target="tpu_custom_call" | custom-call | tf_op jit(solution)/shard_map/state/pallas_call | solution.py:340
  3.8 0.0 copy-start
  3.8 3.1 %collective-permute-start.1 = (f32[2,128,128]{2,1,0:T(8,128)S(1)}, f32[2,128,128]{2,1,0:T(8,128)S(1)}, u32[]{:S(2)}, u32[]{:S(2)}) collective-permute-start(f32[2,128,128]{2,1,0:T(8,128)S(1)} %get-tuple-element.29), channel_id=1, source_target_pairs={{0,16},{8,24},{16,0},{24,8},{1,17},{9,25},{17,1},{25,9},{2,18},{10... | collective-permute-start | bytes 393224 | tf_op jit(solution)/shard_map/ppermute | solution.py:309
  6.9 3.5 %collective-permute-done.1 = f32[2,128,128]{2,1,0:T(8,128)S(1)} collective-permute-done((f32[2,128,128]{2,1,0:T(8,128)S(1)}, f32[2,128,128]{2,1,0:T(8,128)S(1)}, u32[]{:S(2)}, u32[]{:S(2)}) %collective-permute-start.1) | collective-permute-done | bytes 131104 | tf_op jit(solution)/shard_map/ppermute | solution.py:309
  10.4 0.5 %collective-permute-start = (f32[2,128,128]{2,1,0:T(8,128)S(1)}, f32[2,128,128]{2,1,0:T(8,128)S(1)}, u32[]{:S(2)}, u32[]{:S(2)}) collective-permute-start(f32[2,128,128]{2,1,0:T(8,128)S(1)} %get-tuple-element.29), channel_id=1, source_target_pairs={{0,8},{8,0},{16,24},{24,16},{1,9},{9,1},{17,25},{25,17},{2,10},{10... | collective-permute-start | bytes 393224 | tf_op jit(solution)/shard_map/ppermute | solution.py:309
  10.9 0.6 %scale.1.scaled_ref = f32[2,128,2048]{2,1,0:T(8,128)S(1)} custom-call(f32[2,2048,128]{2,1,0:T(8,128)S(1)} %copy-done.1, f32[1,128]{1,0:T(1,128)S(1)} %bitcast.7), custom_call_target="tpu_custom_call" | custom-call | tf_op jit(solution)/shard_map/scale/pallas_call | solution.py:393
  11.5 3.9 %local.1 = (bf16[2,256,2048]{2,1,0:T(8,128)(2,1)S(1)}, bf16[2,256,2048]{2,1,0:T(8,128)(2,1)S(1)}, f32[2,128,2048]{2,1,0:T(8,128)S(1)}) custom-call(f32[3,2,16,128]{3,2,1,0:T(8,128)S(1)} %get-tuple-element.18.weight_ref, f32[2,2048,128]{2,1,0:T(8,128)S(1)} %copy-done, bf16[2,2048,256]{2,1,0:T(8,128)(2,1)S(1)} %get-tuple-element.21.key_ref, ...), custom_call_target="tpu_custom_call" | custom-call | tf_op jit(solution)/shard_map/local/pallas_call | solution.py:379
  15.4 0.0 collective-permute-done.2
  15.4 1.1 %combine.1 = (f32[2,128,2048]{2,1,0:T(8,128)S(1)}, f32[2,2,16,128]{3,2,1,0:T(8,128)S(1)}) custom-call(f32[2,128,2048]{2,1,0:T(8,128)S(1)} %get-tuple-element.24.local_ref, bf16[2,256,2048]{2,1,0:T(8,128)(2,1)S(1)} %get-tuple-element.25.high_ref, bf16[2,256,2048]{2,1,0:T(8,128)(2,1)S(1)} %get-tuple-element.26.low_ref, f32[2,128,2048]{2,1,0:T(8,128)S(1)} %scale.1.scaled_ref, ...), custom_call_target="tpu_custom_call" | custom-call | tf_op jit(solution)/shard_map/combine/pallas_call | solution.py:401
  16.6 2.9 %collective-permute-start.3 = (f32[2,2,16,128]{3,2,1,0:T(8,128)S(1)}, f32[2,2,16,128]{3,2,1,0:T(8,128)S(1)}, u32[]{:S(2)}, u32[]{:S(2)}) collective-permute-start(f32[2,2,16,128]{3,2,1,0:T(8,128)S(1)} %get-tuple-element.30), channel_id=1, source_target_pairs={{0,4},{1,5},{2,6},{3,7},{4,0},{5,1},{6,2},{7,3},{8,12},{9,13},{10,... | collective-permute-start | bytes 98312 | tf_op jit(solution)/shard_map/ppermute | solution.py:314
  19.4 2.0 %collective-permute-done.3 = f32[2,2,16,128]{3,2,1,0:T(8,128)S(1)} collective-permute-done((f32[2,2,16,128]{3,2,1,0:T(8,128)S(1)}, f32[2,2,16,128]{3,2,1,0:T(8,128)S(1)}, u32[]{:S(2)}, u32[]{:S(2)}) %collective-permute-start.3) | collective-permute-done | bytes 32800 | tf_op jit(solution)/shard_map/ppermute | solution.py:314
  21.5 2.1 %collective-permute-start.4 = (f32[2,2,16,128]{3,2,1,0:T(8,128)S(1)}, f32[2,2,16,128]{3,2,1,0:T(8,128)S(1)}, u32[]{:S(2)}, u32[]{:S(2)}) collective-permute-start(f32[2,2,16,128]{3,2,1,0:T(8,128)S(1)} %add.16), channel_id=1, source_target_pairs={{0,1},{1,0},{2,3},{3,2},{4,5},{5,4},{6,7},{7,6},{8,9},{9,8},{10,11... | collective-permute-start | bytes 98312 | tf_op jit(solution)/shard_map/ppermute | solution.py:314
  23.5 1.2 %collective-permute-start.5 = (f32[2,2,16,128]{3,2,1,0:T(8,128)S(1)}, f32[2,2,16,128]{3,2,1,0:T(8,128)S(1)}, u32[]{:S(2)}, u32[]{:S(2)}) collective-permute-start(f32[2,2,16,128]{3,2,1,0:T(8,128)S(1)} %add.16), channel_id=1, source_target_pairs={{0,3},{1,2},{2,1},{3,0},{4,7},{5,6},{6,5},{7,4},{8,11},{9,10},{10,... | collective-permute-start | bytes 98312 | tf_op jit(solution)/shard_map/ppermute | solution.py:314
  24.7 0.3 collective-permute-start.6
  25.1 0.7 %collective-permute-done.4 = f32[2,2,16,128]{3,2,1,0:T(8,128)S(1)} collective-permute-done((f32[2,2,16,128]{3,2,1,0:T(8,128)S(1)}, f32[2,2,16,128]{3,2,1,0:T(8,128)S(1)}, u32[]{:S(2)}, u32[]{:S(2)}) %collective-permute-start.4) | collective-permute-done | bytes 32800 | tf_op jit(solution)/shard_map/ppermute | solution.py:314
  25.8 2.6 %collective-permute-done.5 = f32[2,2,16,128]{3,2,1,0:T(8,128)S(1)} collective-permute-done((f32[2,2,16,128]{3,2,1,0:T(8,128)S(1)}, f32[2,2,16,128]{3,2,1,0:T(8,128)S(1)}, u32[]{:S(2)}, u32[]{:S(2)}) %collective-permute-start.5) | collective-permute-done | bytes 32800 | tf_op jit(solution)/shard_map/ppermute | solution.py:314
  28.3 0.3 collective-permute-done.6
  28.6 0.9 %top_gradient.1 = (f32[2,128,128]{2,1,0:T(8,128)S(1)}, bf16[2,256,2048]{2,1,0:T(8,128)(2,1)S(1)}) custom-call(f32[2,2,16,128]{3,2,1,0:T(8,128)S(1)} %add_add_fusion.sums_ref, f32[2,128,2048]{2,1,0:T(8,128)S(1)} %get-tuple-element.31.combined_ref, f32[2,128,2048]{2,1,0:T(8,128)S(1)} %scale.1.scaled_ref, bf16[2,256,2048]{2,1,0:T(8,128)(2,1)S(1)} %get-tuple-element.25.high_ref, ...), custom_call_target="tpu_custom_call" | custom-call | tf_op jit(solution)/shard_map/top_gradient/pallas_call | solution.py:418
  29.6 1.6 %collective-permute-start.7 = (f32[2,128,128]{2,1,0:T(8,128)S(1)}, f32[2,128,128]{2,1,0:T(8,128)S(1)}, u32[]{:S(2)}, u32[]{:S(2)}) collective-permute-start(f32[2,128,128]{2,1,0:T(8,128)S(1)} %get-tuple-element.32), channel_id=1, source_target_pairs={{0,16},{8,24},{16,0},{24,8},{1,17},{9,25},{17,1},{25,9},{2,18},{10... | collective-permute-start | bytes 393224 | tf_op jit(solution)/shard_map/ppermute | solution.py:309
  31.2 0.8 %rest_gradient.1 = f32[2,128,128]{2,1,0:T(8,128)S(1)} custom-call(bf16[2,256,2048]{2,1,0:T(8,128)(2,1)S(1)} %get-tuple-element.33.parts_ref, bf16[2,256,2048]{2,1,0:T(8,128)(2,1)S(1)} %get-tuple-element.25.high_ref, bf16[2,256,2048]{2,1,0:T(8,128)(2,1)S(1)} %get-tuple-element.26.low_ref), custom_call_target="tpu_custom_call" | custom-call | tf_op jit(solution)/shard_map/rest_gradient/pallas_call | solution.py:425
  32.0 0.1 collective-permute-start.9
  32.1 2.6 %collective-permute-done.7.refs_0_ = f32[2,128,128]{2,1,0:T(8,128)S(1)} collective-permute-done((f32[2,128,128]{2,1,0:T(8,128)S(1)}, f32[2,128,128]{2,1,0:T(8,128)S(1)}, u32[]{:S(2)}, u32[]{:S(2)}) %collective-permute-start.7) | collective-permute-done | bytes 131104 | tf_op jit(solution)/shard_map/ppermute | solution.py:309
  34.6 1.7 %attended.1 = f32[2,2048,128]{2,1,0:T(8,128)} custom-call(f32[2,2,16,128]{3,2,1,0:T(8,128)S(1)} %add_add_fusion.sums_ref, f32[2,128,2048]{2,1,0:T(8,128)S(1)} %get-tuple-element.31.combined_ref, f32[1,128]{1,0:T(1,128)S(1)} %bitcast.8), custom_call_target="tpu_custom_call" | custom-call | tf_op jit(solution)/shard_map/attended/pallas_call | solution.py:433
  36.3 0.7 %finish.1 = f32[2,128,128]{2,1,0:T(8,128)} custom-call(f32[2,128,128]{2,1,0:T(8,128)S(1)} %collective-permute-done.7.refs_0_, f32[2,128,128]{2,1,0:T(8,128)S(1)} %collective-permute-done.8.refs_1_, f32[2,128,128]{2,1,0:T(8,128)S(1)} %collective-permute-done.9.refs_2_), custom_call_target="tpu_custom_call" | custom-call | tf_op jit(solution)/shard_map/finish/pallas_call | solution.py:451
  (13 shorter events, 0.1 us)
Async XLA Ops:
  0.6 10.3 %copy-start.1 = (f32[2,2048,128]{2,1,0:T(8,128)S(1)}, f32[2,2048,128]{2,1,0:T(8,128)}, u32[]{:S(2)}) copy-start(f32[2,2048,128]{2,1,0:T(8,128)} %cotangent_ref) | copy-start | bytes 6291460
  0.6 10.2 %copy-start.2 = (f32[128]{0:T(128)S(1)}, f32[128]{0:T(128)}, u32[]{:S(2)}) copy-start(f32[128]{0:T(128)} %param.15) | copy-start | bytes 1540
  3.8 7.7 %copy-start = (f32[2,2048,128]{2,1,0:T(8,128)S(1)}, f32[2,2048,128]{2,1,0:T(8,128)}, u32[]{:S(2)}) copy-start(f32[2,2048,128]{2,1,0:T(8,128)} %query_ref) | copy-start | bytes 6291460
  3.8 6.6 %collective-permute-start.1 = (f32[2,128,128]{2,1,0:T(8,128)S(1)}, f32[2,128,128]{2,1,0:T(8,128)S(1)}, u32[]{:S(2)}, u32[]{:S(2)}) collective-permute-start(f32[2,128,128]{2,1,0:T(8,128)S(1)} %get-tuple-element.29), channel_id=1, source_target_pairs={{0,16},{8,24},{16,0},{24,8},{1,17},{9,25},{17,1},{25,9},{2,18},{10... | collective-permute-start | bytes 393224 | tf_op jit(solution)/shard_map/ppermute | solution.py:309
  10.4 5.0 %collective-permute-start.2 = (f32[2,128,128]{2,1,0:T(8,128)S(1)}, f32[2,128,128]{2,1,0:T(8,128)S(1)}, u32[]{:S(2)}, u32[]{:S(2)}) collective-permute-start(f32[2,128,128]{2,1,0:T(8,128)S(1)} %collective-permute-done.1), channel_id=1, source_target_pairs={{0,8},{8,0},{16,24},{24,16},{1,9},{9,1},{17,25},{25,17},{2,10},{10... | collective-permute-start | bytes 393224 | tf_op jit(solution)/shard_map/ppermute | solution.py:309
  10.4 5.1 %collective-permute-start = (f32[2,128,128]{2,1,0:T(8,128)S(1)}, f32[2,128,128]{2,1,0:T(8,128)S(1)}, u32[]{:S(2)}, u32[]{:S(2)}) collective-permute-start(f32[2,128,128]{2,1,0:T(8,128)S(1)} %get-tuple-element.29), channel_id=1, source_target_pairs={{0,8},{8,0},{16,24},{24,16},{1,9},{9,1},{17,25},{25,17},{2,10},{10... | collective-permute-start | bytes 393224 | tf_op jit(solution)/shard_map/ppermute | solution.py:309
  16.6 4.9 %collective-permute-start.3 = (f32[2,2,16,128]{3,2,1,0:T(8,128)S(1)}, f32[2,2,16,128]{3,2,1,0:T(8,128)S(1)}, u32[]{:S(2)}, u32[]{:S(2)}) collective-permute-start(f32[2,2,16,128]{3,2,1,0:T(8,128)S(1)} %get-tuple-element.30), channel_id=1, source_target_pairs={{0,4},{1,5},{2,6},{3,7},{4,0},{5,1},{6,2},{7,3},{8,12},{9,13},{10,... | collective-permute-start | bytes 98312 | tf_op jit(solution)/shard_map/ppermute | solution.py:314
  21.5 4.3 %collective-permute-start.4 = (f32[2,2,16,128]{3,2,1,0:T(8,128)S(1)}, f32[2,2,16,128]{3,2,1,0:T(8,128)S(1)}, u32[]{:S(2)}, u32[]{:S(2)}) collective-permute-start(f32[2,2,16,128]{3,2,1,0:T(8,128)S(1)} %add.16), channel_id=1, source_target_pairs={{0,1},{1,0},{2,3},{3,2},{4,5},{5,4},{6,7},{7,6},{8,9},{9,8},{10,11... | collective-permute-start | bytes 98312 | tf_op jit(solution)/shard_map/ppermute | solution.py:314
  23.5 4.8 %collective-permute-start.5 = (f32[2,2,16,128]{3,2,1,0:T(8,128)S(1)}, f32[2,2,16,128]{3,2,1,0:T(8,128)S(1)}, u32[]{:S(2)}, u32[]{:S(2)}) collective-permute-start(f32[2,2,16,128]{3,2,1,0:T(8,128)S(1)} %add.16), channel_id=1, source_target_pairs={{0,3},{1,2},{2,1},{3,0},{4,7},{5,6},{6,5},{7,4},{8,11},{9,10},{10,... | collective-permute-start | bytes 98312 | tf_op jit(solution)/shard_map/ppermute | solution.py:314
  24.7 3.9 %collective-permute-start.6 = (f32[2,2,16,128]{3,2,1,0:T(8,128)S(1)}, f32[2,2,16,128]{3,2,1,0:T(8,128)S(1)}, u32[]{:S(2)}, u32[]{:S(2)}) collective-permute-start(f32[2,2,16,128]{3,2,1,0:T(8,128)S(1)} %add.16), channel_id=1, source_target_pairs={{0,2},{1,3},{2,0},{3,1},{4,6},{5,7},{6,4},{7,5},{8,10},{9,11},{10,... | collective-permute-start | bytes 98312 | tf_op jit(solution)/shard_map/ppermute | solution.py:314
  29.6 5.0 %collective-permute-start.7 = (f32[2,128,128]{2,1,0:T(8,128)S(1)}, f32[2,128,128]{2,1,0:T(8,128)S(1)}, u32[]{:S(2)}, u32[]{:S(2)}) collective-permute-start(f32[2,128,128]{2,1,0:T(8,128)S(1)} %get-tuple-element.32), channel_id=1, source_target_pairs={{0,16},{8,24},{16,0},{24,8},{1,17},{9,25},{17,1},{25,9},{2,18},{10... | collective-permute-start | bytes 393224 | tf_op jit(solution)/shard_map/ppermute | solution.py:309
  32.0 4.3 %collective-permute-start.9 = (f32[2,128,128]{2,1,0:T(8,128)S(1)}, f32[2,128,128]{2,1,0:T(8,128)S(1)}, u32[]{:S(2)}, u32[]{:S(2)}) collective-permute-start(f32[2,128,128]{2,1,0:T(8,128)S(1)} %rest_gradient.1), channel_id=1, source_target_pairs={{0,8},{8,0},{16,24},{24,16},{1,9},{9,1},{17,25},{25,17},{2,10},{10... | collective-permute-start | bytes 393224 | tf_op jit(solution)/shard_map/ppermute | solution.py:309
  34.6 1.7 %collective-permute-start.8 = (f32[2,128,128]{2,1,0:T(8,128)S(1)}, f32[2,128,128]{2,1,0:T(8,128)S(1)}, u32[]{:S(2)}, u32[]{:S(2)}) collective-permute-start(f32[2,128,128]{2,1,0:T(8,128)S(1)} %collective-permute-done.7.refs_0_), channel_id=1, source_target_pairs={{0,8},{8,0},{16,24},{24,16},{1,9},{9,1},{17,25},{25,17},{2,10},{10... | collective-permute-start | bytes 393224 | tf_op jit(solution)/shard_map/ppermute | solution.py:309
